TPU v7x, 128 devices: a whole 4x4x4 slice. The times are simulated.
128 devices in a mesh: grp: 64 (over z, y, x), sub: 2 (over core).
Axes of the slice: x: 4, y: 4, z: 4, core: 2. Of those that a mesh axis runs over, the one named last changes fastest.
Arguments:
- potentials: bfloat16 [4096, 200, 200], P(('grp', 'sub')), may hold values from -6 to 6
- dimers: int32 [16384, 2], P(('grp', 'sub')), may hold values from 0 to 4095, as said below
- coupling: float32 [16384], P(('grp', 'sub')), may hold values from 0.3 to 1.5
- transform: bfloat16 [400, 400], replicated, may hold values from -0.3125 to 0.3125
Outputs:
- energies: float32 [16384, 400], P(('grp', 'sub'))
- checksum: float32 [1], replicated
Inputs may be any that keep to these rules, and one draw needn't show every extreme that they name: `dimers`: each row names two different fragments. Rows d with d // 128 = o belong to owner o, and their second fragment f has f // 32 = o. Among the 128 first fragments of one owner's rows, at most 2 fall into the fragments of any one device (fragments f with f // 32 equal), and exactly 2 into some device's fragments.
All inputs are finite; a program needn't handle non-finite values.
Results may differ from a plain program's by a relative error of at most 0.0023.
Values may be sent and summed in bfloat16 or wider, within the bound.
A program may use at most 192 MiB of HBM per device.

v0:
```python
import jax
import jax.numpy as jnp
from jax import lax
from jax.sharding import Mesh
from jax.sharding import PartitionSpec as P

GRP_SUB = ("grp_0", "grp_1", "grp_2", "sub")


def in_blocks(value, dim, peers):
    before, after = (value.shape[:dim], value.shape[dim + 1 :])
    return jnp.moveaxis(value.reshape(*before, peers, -1, *after), dim, 0)


def edges_of(length, count):
    unit = 8 if length >= 8 * count else 1
    return [length // unit * k // count * unit for k in range(1, count)]


def in_order(tiles, dim):
    tiles = jnp.moveaxis(tiles, 0, dim)
    shape = tiles.shape
    return tiles.reshape(*shape[:dim], shape[dim] * shape[dim + 1], *shape[dim + 2 :])


def several_exchanges(value, axis, pieces, split_dim, concat_dim):
    tiles = in_blocks(value, split_dim, lax.axis_size(axis))
    widest = max(range(1, max(2, tiles.ndim - 1)), key=lambda d: tiles.shape[d])
    done = []
    for section in jnp.split(tiles, edges_of(tiles.shape[widest], pieces), axis=widest):
        if section.size:
            done.append(lax.all_to_all(section, axis, split_axis=0, concat_axis=0, tiled=True))
    return in_order(jnp.concatenate(done, axis=widest), concat_dim)


def over_axes(value, axes):
    for axis in axes:
        value = lax.psum(value, axis)
    return value


def block_energies(left, right, scale, transform, basis):
    upper = transform[:basis]
    lower = transform[basis:]
    cross = jnp.einsum("nab,nbc->nac", left, right, preferred_element_type=jnp.float32)
    block = (cross * (scale[:, None, None] / jnp.sqrt(jnp.float32(basis)))).astype(jnp.bfloat16)
    top = jnp.einsum("nab,bk->nak", left, upper, preferred_element_type=jnp.float32)
    top = top + jnp.einsum("nab,bk->nak", block, lower, preferred_element_type=jnp.float32)
    bottom = jnp.einsum("nab,ak->nbk", block, upper, preferred_element_type=jnp.float32)
    bottom = bottom + jnp.einsum("nab,bk->nak", right, lower, preferred_element_type=jnp.float32)
    upper_f = upper.astype(jnp.float32)
    lower_f = lower.astype(jnp.float32)
    return jnp.sum(upper_f[None] * top, axis=1) + jnp.sum(lower_f[None] * bottom, axis=1)


def local(potentials, dimers, coupling, transform):
    frag_dev, basis, _ = potentials.shape
    count = dimers.shape[0]
    owners = lax.axis_size(GRP_SUB)
    cap = max(2, (4 * count + 3 * owners - 1) // (3 * owners))
    wanted = dimers[:, 0]
    source = wanted // frag_dev
    onehot = (source[:, None] == jnp.arange(owners, dtype=jnp.int32)[None, :]).astype(jnp.int32)
    ranking = jnp.sum(jnp.cumsum(onehot, axis=0) * onehot, axis=1) - 1
    slots = source * cap + ranking
    requests = jnp.zeros((owners * cap,), jnp.int32).at[slots].set(wanted % frag_dev)
    asked = lax.all_to_all(
        requests.reshape(owners, cap), GRP_SUB, split_axis=0, concat_axis=0, tiled=True
    )
    served = jnp.take(potentials, asked.reshape(-1), axis=0).reshape(owners, cap, basis, basis)
    arrived = several_exchanges(served, GRP_SUB, 2, 0, 0)
    leading = jnp.take(arrived.reshape(owners * cap, basis, basis), slots, axis=0)
    trailing = jnp.take(potentials, dimers[:, 1] % frag_dev, axis=0)
    width = 8
    leading = leading.reshape(count // width, width, basis, basis)
    trailing = trailing.reshape(count // width, width, basis, basis)
    scales = coupling.reshape(count // width, width)

    def one_block(item):
        left, right, scale = item
        return block_energies(left, right, scale, transform, basis)

    energies = lax.map(one_block, (leading, trailing, scales)).reshape(count, 2 * basis)
    total = count * owners
    position = lax.axis_index(GRP_SUB) * count + jnp.arange(count, dtype=jnp.int32)
    weights = (position.astype(jnp.float32) + 1.0) / total
    partial_value = 2.0 / total * jnp.sum(weights * jnp.mean(energies * energies, axis=1))
    checksum = over_axes(partial_value, GRP_SUB)
    return (energies, checksum.reshape(1))


def solution(mesh):
    split = Mesh(
        mesh.devices.reshape(4, 4, 4, mesh.shape["sub"]), ("grp_0", "grp_1", "grp_2", "sub")
    )
    return jax.shard_map(
        local,
        mesh=split,
        in_specs=(P(GRP_SUB, None, None), P(GRP_SUB, None), P(GRP_SUB), P()),
        out_specs=(P(GRP_SUB, None), P()),
        check_vma=False,
    )
```

profile of v0, /device:TPU:1, one launch (start us, length us, event | category | flops | bytes accessed | tf_op | source)
XLA Modules:
  0.0 635.7 jit_solution(10583920919584439760)
XLA Ops:
  5.2 20.9 %all_to_all.19 = s32[128,1,2]{2,1,0:T(1,128)S(1)} all-to-all(s32[128,1,2]{2,1,0:T(1,128)S(1)} %bitcast.76), channel_id=1, replica_groups=mesh['grp_0'=4,'grp_1'=4,'grp_2'=4,'sub'=2] {'grp_0','grp_1','grp_2','sub'}, dimensions={0} | all-to-all | bytes 2048 | tf_op jit(solution)/shard_map/all_to_all | solution.py:67
  27.8 12.6 %gather_fusion = bf16[256,200,200]{2,1,0:T(8,128)(2,1)} fusion(bf16[32,200,200]{2,1,0:T(8,128)(2,1)S(1)} %copy-done, s32[1024]{0:T(1024)S(1)} %pad_clamp_fusion.2), kind=kCustom, calls=%fused_computation | custom fusion | bytes 40961024 | tf_op jit(solution)/shard_map/jit(_take)/gather | solution.py:70
  40.3 18.3 %broadcast_select_fusion = bf16[128,1,2,200,200]{4,3,2,1,0:T(8,128)(2,1)} fusion(bf16[128,1,2,200,200]{4,3,2,1,0:T(8,128)(2,1)} %bitcast.70, pred[128,2]{1,0:T(8,128)(4,1)S(1)} %compare_and_fusion), kind=kLoop, calls=%fused_computation.35 | loop fusion | flops 10240000 | bytes 40960256 | tf_op jit(solution)/shard_map/jit(_take)/select_n | solution.py:70
  58.7 11.0 %split.8 = bf16[128,1,2,96,200]{4,3,2,1,0:T(8,128)(2,1)} slice(bf16[128,1,2,200,200]{4,3,2,1,0:T(8,128)(2,1)} %broadcast_select_fusion), slice={[0:128], [0:1], [0:2], [0:96], [0:200]} | slice | bytes 19660800 | tf_op jit(solution)/shard_map/split | solution.py:30
  69.6 5.5 all-to-all-start.1
  75.1 12.2 %split.9 = bf16[128,1,2,104,200]{4,3,2,1,0:T(8,128)(2,1)} slice(bf16[128,1,2,200,200]{4,3,2,1,0:T(8,128)(2,1)} %broadcast_select_fusion), slice={[0:128], [0:1], [0:2], [96:200], [0:200]} | slice | bytes 21299200 | tf_op jit(solution)/shard_map/split | solution.py:30
  87.2 18.8 %copy.31 = bf16[128,1,2,104,200]{3,4,2,1,0:T(8,128)(2,1)} copy(bf16[128,1,2,104,200]{4,3,2,1,0:T(8,128)(2,1)} %split.9) | data formatting | bytes 21299200 | tf_op jit(solution)/shard_map/split | solution.py:30
  106.1 121.2 %all-to-all-done.1 = bf16[128,1,2,96,200]{4,3,2,1,0:T(8,128)(2,1)} async-done(((bf16[128,1,2,96,200]{4,3,2,1,0:T(8,128)(2,1)}), bf16[128,1,2,96,200]{4,3,2,1,0:T(8,128)(2,1)}, u32[]{:S(2)}, u32[]{:S(2)}) %all-to-all-start.1) | async-done | bytes 9830432 | tf_op jit(solution)/shard_map/all_to_all | solution.py:32
  227.3 24.5 %all-to-all-start.2 = ((bf16[128,1,2,104,200]{3,4,2,1,0:T(8,128)(2,1)}), bf16[128,1,2,104,200]{3,4,2,1,0:T(8,128)(2,1)}, u32[]{:S(2)}, u32[]{:S(2)}) async-start(bf16[128,1,2,104,200]{3,4,2,1,0:T(8,128)(2,1)} %copy.31), calls=%async_computation.2 | async-start | bytes 26214400 | tf_op jit(solution)/shard_map/all_to_all | solution.py:32
  252.6 8.7 %gather_fusion.2 = bf16[128,200,200]{2,1,0:T(8,128)(2,1)} fusion(bf16[32,200,200]{2,1,0:T(8,128)(2,1)S(1)} %copy-done, s32[1024]{0:T(1024)S(1)} %pad_clamp_fusion), kind=kCustom, calls=%fused_computation.2 | custom fusion | bytes 20480512 | tf_op jit(solution)/shard_map/jit(_take)/gather | solution.py:73
  262.1 10.1 %broadcast_select_fusion.1 = bf16[16,8,200,200]{3,2,1,0:T(8,128)(2,1)} fusion(bf16[16,8,200,200]{3,2,1,0:T(8,128)(2,1)} %bitcast.73, pred[16,8]{1,0:T(8,128)(4,1)S(1)} %broadcast_in_dim.59), kind=kLoop, calls=%fused_computation.36 | loop fusion | flops 5120000 | bytes 20480128 | tf_op jit(solution)/shard_map/jit(_take)/select_n | solution.py:73
  272.2 17.3 %copy.32 = bf16[128,1,2,96,200]{3,4,2,1,0:T(8,128)(2,1)} copy(bf16[128,1,2,96,200]{4,3,2,1,0:T(8,128)(2,1)} %all-to-all-done.1) | data formatting | bytes 19660800 | tf_op jit(solution)/shard_map/all_to_all | solution.py:32
  289.6 123.4 %all-to-all-done.2 = bf16[128,1,2,104,200]{3,4,2,1,0:T(8,128)(2,1)} async-done(((bf16[128,1,2,104,200]{3,4,2,1,0:T(8,128)(2,1)}), bf16[128,1,2,104,200]{3,4,2,1,0:T(8,128)(2,1)}, u32[]{:S(2)}, u32[]{:S(2)}) %all-to-all-start.2) | async-done | bytes 10649632 | tf_op jit(solution)/shard_map/all_to_all | solution.py:32
  413.0 18.7 %pad_maximum_fusion = bf16[128,1,2,200,200]{3,4,2,1,0:T(8,128)(2,1)} fusion(bf16[128,1,2,104,200]{3,4,2,1,0:T(8,128)(2,1)} %all-to-all-done.2, bf16[128,1,2,96,200]{3,4,2,1,0:T(8,128)(2,1)} %copy.32), kind=kLoop, calls=%fused_computation.34 | loop fusion | flops 40960000 | bytes 40960000 | tf_op jit(solution)/shard_map/concatenate | solution.py:33
  431.7 17.1 %gather_fusion.1 = bf16[128,200,200]{1,2,0:T(8,128)(2,1)} fusion(bf16[256,200,200]{1,2,0:T(8,128)(2,1)} %bitcast.71, s32[1024]{0:T(1024)S(1)} %pad_clamp_fusion.1), kind=kCustom, calls=%fused_computation.1 | custom fusion | bytes 20480512 | tf_op jit(solution)/shard_map/jit(_take)/gather | solution.py:72
  448.8 17.9 %copy.33 = bf16[128,200,200]{2,1,0:T(8,128)(2,1)} copy(bf16[128,200,200]{1,2,0:T(8,128)(2,1)} %gather_fusion.1) | data formatting | bytes 20480000 | tf_op jit(solution)/shard_map/jit(_take)/gather | solution.py:72
  466.7 10.3 %broadcast_select_fusion.2 = bf16[16,8,200,200]{3,2,1,0:T(8,128)(2,1)} fusion(bf16[16,8,200,200]{3,2,1,0:T(8,128)(2,1)} %bitcast.72, pred[16,8]{1,0:T(8,128)(4,1)S(1)} %broadcast_in_dim.51), kind=kLoop, calls=%fused_computation.37 | loop fusion | flops 5120000 | bytes 20480128 | tf_op jit(solution)/shard_map/jit(_take)/select_n | solution.py:72
  477.0 110.3 %while.10 = (s32[]{:T(128)}, f32[16,8,400]{2,1,0:T(8,128)S(1)}, bf16[400,400]{1,0:T(8,128)(2,1)S(1)}, bf16[16,8,200,200]{3,2,1,0:T(8,128)(2,1)}, bf16[16,8,200,2...) while((s32[]{:T(128)}, f32[16,8,400]{2,1,0:T(8,128)S(1)}, bf16[400,400]{1,0:T(8,128)(2,1)S(1)}, ...), condition=%wide.region_6.7_spmd, body=%wide.region_3.6_spmd.sunk | while | flops 1156636800 | bytes 19904180 | solution.py:83
  482.0 1.9 multiply_reduce_fusion.7
  483.9 1.8 multiply_convert_fusion.2
  488.9 1.9 multiply_reduce_fusion.7
  490.8 1.8 multiply_convert_fusion.2
  495.8 1.9 multiply_reduce_fusion.7
  497.7 1.8 multiply_convert_fusion.2
  502.7 1.9 multiply_reduce_fusion.7
  504.6 1.8 multiply_convert_fusion.2
  509.6 1.9 multiply_reduce_fusion.7
  511.5 1.8 multiply_convert_fusion.2
  516.5 1.9 multiply_reduce_fusion.7
  523.4 1.9 multiply_reduce_fusion.7
  530.3 1.9 multiply_reduce_fusion.7
  537.1 1.9 multiply_reduce_fusion.7
  539.1 1.8 multiply_convert_fusion.2
  544.0 1.9 multiply_reduce_fusion.7
  546.0 1.8 multiply_convert_fusion.2
  550.9 1.9 multiply_reduce_fusion.7
  552.9 1.8 multiply_convert_fusion.2
  557.8 1.9 multiply_reduce_fusion.7
  559.7 1.8 multiply_convert_fusion.2
  564.7 1.9 multiply_reduce_fusion.7
  566.6 1.8 multiply_convert_fusion.2
  571.6 1.9 multiply_reduce_fusion.7
  578.5 1.9 multiply_reduce_fusion.7
  585.4 1.9 multiply_reduce_fusion.7
  589.0 11.9 %psum.28 = f32[]{:T(128)} all-reduce(f32[]{:T(128)S(6)} %mul_shard_map.3), channel_id=1, replica_groups=mesh['grp_0'=4,'grp_1'=4,'grp_2'=4,'sub'=2] {'grp_0'}, use_global_device_ids=true, to_apply=%region_9.10 | all-reduce | flops 1 | bytes 8 | tf_op jit(solution)/shard_map/psum | solution.py:38
  600.8 13.8 %psum.29 = f32[]{:T(128)} all-reduce(f32[]{:T(128)} %psum.28), channel_id=1, replica_groups=mesh['grp_0'=4,'grp_1'=4,'grp_2'=4,'sub'=2] {'grp_1'}, use_global_device_ids=true, to_apply=%region_10.11 | all-reduce | flops 1 | bytes 8 | tf_op jit(solution)/shard_map/psum | solution.py:38
  614.6 11.1 %psum.30 = f32[]{:T(128)} all-reduce(f32[]{:T(128)} %psum.29), channel_id=1, replica_groups=mesh['grp_0'=4,'grp_1'=4,'grp_2'=4,'sub'=2] {'grp_2'}, use_global_device_ids=true, to_apply=%region_11.12 | all-reduce | flops 1 | bytes 8 | tf_op jit(solution)/shard_map/psum | solution.py:38
  625.7 9.2 %psum.31 = f32[1]{0:T(128)} all-reduce(f32[1]{0:T(128)} %bitcast.19), channel_id=1, replica_groups=mesh['grp_0'=4,'grp_1'=4,'grp_2'=4,'sub'=2] {'sub'}, use_global_device_ids=true, to_apply=%region_12.13 | all-reduce | flops 1 | bytes 8 | tf_op jit(solution)/shard_map/psum | solution.py:38
  (132 shorter events, 71.2 us)
Async XLA Ops:
  0.6 27.1 %copy-start = (bf16[32,200,200]{2,1,0:T(8,128)(2,1)S(1)}, bf16[32,200,200]{2,1,0:T(8,128)(2,1)}, u32[]{:S(2)}) copy-start(bf16[32,200,200]{2,1,0:T(8,128)(2,1)} %param.6) | copy-start | bytes 7680004
  69.6 157.7 %all-to-all-start.1 = ((bf16[128,1,2,96,200]{4,3,2,1,0:T(8,128)(2,1)}), bf16[128,1,2,96,200]{4,3,2,1,0:T(8,128)(2,1)}, u32[]{:S(2)}, u32[]{:S(2)}) async-start(bf16[128,1,2,96,200]{4,3,2,1,0:T(8,128)(2,1)} %split.8), calls=%async_computation.1 | async-start | bytes 25165824 | tf_op jit(solution)/shard_map/all_to_all | solution.py:32
  227.3 185.7 %all-to-all-start.2 = ((bf16[128,1,2,104,200]{3,4,2,1,0:T(8,128)(2,1)}), bf16[128,1,2,104,200]{3,4,2,1,0:T(8,128)(2,1)}, u32[]{:S(2)}, u32[]{:S(2)}) async-start(bf16[128,1,2,104,200]{3,4,2,1,0:T(8,128)(2,1)} %copy.31), calls=%async_computation.2 | async-start | bytes 26214400 | tf_op jit(solution)/shard_map/all_to_all | solution.py:32
  466.7 10.3 %copy-start.2 = (bf16[400,400]{1,0:T(8,128)(2,1)S(1)}, bf16[400,400]{1,0:T(8,128)(2,1)}, u32[]{:S(2)}) copy-start(bf16[400,400]{1,0:T(8,128)(2,1)} %param.9) | copy-start | bytes 960004
  587.3 48.4 %copy-start.1 = (bf16[32,200,200]{2,1,0:T(8,128)(2,1)S(1)}, bf16[32,200,200]{2,1,0:T(8,128)(2,1)}, u32[]{:S(2)}) copy-start(bf16[32,200,200]{2,1,0:T(8,128)(2,1)} %param.6) | copy-start | bytes 7680004
where the time goes:
time: 639 us; the launch traced here: 636 us
  waiting for transfers between devices  245 us (38%)
  local copies, waits for them, and re-layouts  119 us (19%)
  matrix products  108 us (17%)
  blocking collectives  66.9 us (10%)
  other arithmetic  64.7 us (10%)
  starting transfers between devices  29.9 us (5%)
    all_to_all x2, waiting for transfers between devices, several_exchanges(): lax.all_to_all(section, axis, split_axis=0, concat_axis=0, tiled=True)  245 us
    psum x4, blocking collectives, over_axes(): value = lax.psum(value, axis)  45.9 us
    split x3, local copies, waits for them, and re-layouts, several_exchanges(): jnp.split(tiles, edges_of(tiles.shape[widest], pieces), axis=widest)  41.9 us
    gather x2, local copies, waits for them, and re-layouts, local(): jnp.take(arrived.reshape(owners * cap, basis, basis), slots, axis=0)  35 us
    all_to_all x2, starting transfers between devices, several_exchanges(): lax.all_to_all(section, axis, split_axis=0, concat_axis=0, tiled=True)  29.9 us
    dot_general x16, matrix products, block_energies(): jnp.einsum('nab,bk->nak', right, lower, preferred_element_type=jnp.float32)  29.7 us
    dot_general x16, matrix products, block_energies(): jnp.einsum('nab,nbc->nac', left, right, preferred_element_type=jnp.float32)  28.3 us
    dot_general x16, matrix products, block_energies(): jnp.einsum('nab,bk->nak', left, upper, preferred_element_type=jnp.float32)  27.7 us
  transfers between devices with their start and end apart: 2, of which 2 were waited for; matrix products, arithmetic and copies ran while one was open for 11% of the time, Pallas kernels for 0%

commit v1 on v0

v1 whole, which is shorter than its diff:
```python
import functools
import math
import jax, jax.numpy as jnp
from jax import lax
from jax.experimental import pallas as pl
from jax.experimental.pallas import tpu as pltpu
from jax.sharding import Mesh
from jax.sharding import PartitionSpec as P

MESH = pl.DeviceIdType.MESH
ROWS = 2544
HALF = 1280
NCOPY = 56

def route_kernel(lq, rq, lg, rg, rel_l, rel_r, bounce, send, recv, loc):
    z, y, x, c = (lax.axis_index(n) for n in ("grp_0", "grp_1", "grp_2", "sub"))

    def dev(dz=0, dy=0, dx=0, dc=0):
        return (lax.rem(z + dz, 4), lax.rem(y + dy, 4), lax.rem(x + dx, 4), lax.rem(c + dc, 2))

    barrier = pltpu.get_barrier_semaphore()
    partners = [dev(dx=1), dev(dx=3), dev(dy=1), dev(dy=3), dev(dz=1), dev(dz=3), dev(dc=1)]
    for p in partners:
        pl.semaphore_signal(barrier, inc=1, device_id=p, device_id_type=MESH)
    pl.semaphore_wait(barrier, len(partners))

    copies = {}

    def send_to(name, src, dst, to):
        i = len(copies)
        copy = pltpu.make_async_remote_copy(
            src_ref=src, dst_ref=dst, send_sem=send.at[i], recv_sem=recv.at[i],
            device_id=to, device_id_type=MESH)
        copy.start()
        copies[name] = copy

    got = lambda *names: [copies[n].wait_recv() for n in names]
    part = lambda d: lax.rem(x + d, 4)
    lo, hi = pl.ds(0, HALF), pl.ds(HALF, ROWS - HALF)

    def ring(dx):
        l_src = lq.at[x] if dx == 0 else lg.at[0, dx]
        r_src = rq.at[x] if dx == 0 else rg.at[0, 0, dx]
        send_to(("z+", dx), l_src, lg.at[3, dx], dev(dz=1))
        send_to(("z-", dx), l_src, lg.at[1, dx], dev(dz=3))
        send_to(("y+", dx), r_src, rg.at[0, 3, dx], dev(dy=1))
        send_to(("y-", dx), r_src, rg.at[0, 1, dx], dev(dy=3))
        send_to(("c", 0, dx), r_src, rg.at[1, 0, dx], dev(dc=1))

    def relay(dx):
        got(("z+", dx))
        send_to(("zr+", dx), lg.at[3, dx, lo], lg.at[2, dx, lo], dev(dz=1))
        got(("z-", dx))
        send_to(("zr-", dx), lg.at[1, dx, hi], lg.at[2, dx, hi], dev(dz=3))
        got(("y+", dx))
        send_to(("yr+", dx), rg.at[0, 3, dx, lo], rg.at[0, 2, dx, lo], dev(dy=1))
        send_to(("c", 3, dx), rg.at[0, 3, dx], rg.at[1, 3, dx], dev(dc=1))
        got(("y-", dx))
        send_to(("yr-", dx), rg.at[0, 1, dx, hi], rg.at[0, 2, dx, hi], dev(dy=3))
        send_to(("c", 1, dx), rg.at[0, 1, dx], rg.at[1, 1, dx], dev(dc=1))

    def last(dx):
        got(("yr+", dx), ("yr-", dx))
        send_to(("c", 2, dx), rg.at[0, 2, dx], rg.at[1, 2, dx], dev(dc=1))
        got(("zr+", dx), ("zr-", dx))

    send_to(("xl", 3), lq.at[part(1)], lg.at[0, 3], dev(dx=1))
    send_to(("xr", 1), rq.at[part(3)], rg.at[0, 0, 1], dev(dx=3))
    ring(0)
    send_to(("xr", 3), rq.at[part(1)], rg.at[0, 0, 3], dev(dx=1))
    send_to(("xl", 1), lq.at[part(3)], lg.at[0, 1], dev(dx=3))
    send_to("l_rel", lq.at[part(2)], rel_l, dev(dx=1))
    send_to("r_rel", rq.at[part(2)], rel_r, dev(dx=3))
    own = [(lq, lg.at[0, 0]), (rq, rg.at[0, 0, 0])]
    for k, (src, dst) in enumerate(own):
        into = pltpu.make_async_copy(src.at[x], bounce.at[k], loc.at[k])
        into.start()
        into.wait()
        out = pltpu.make_async_copy(bounce.at[k], dst, loc.at[2 + k])
        out.start()
        own[k] = out
    relay(0)
    got(("xl", 3), ("xr", 3))
    ring(3)
    got(("xl", 1), ("xr", 1))
    ring(1)
    got("l_rel")
    send_to(("xl", 2), rel_l, lg.at[0, 2], dev(dx=1))
    got("r_rel")
    send_to(("xr", 2), rel_r, rg.at[0, 0, 2], dev(dx=3))
    last(0)
    relay(3)
    got(("xl", 2), ("xr", 2))
    ring(2)
    relay(1)
    last(3)
    last(1)
    relay(2)
    last(2)
    for dx in range(4):
        for dy in range(4):
            copies[("c", dy, dx)].wait_recv()
    for out in own:
        out.wait()
    for copy in copies.values():
        copy.wait_send()
    assert len(copies) == NCOPY


def route(lq, rq):
    blk = (ROWS, 128)
    any_ = pl.BlockSpec(memory_space=pl.ANY)
    bf = jnp.bfloat16
    return pl.pallas_call(
        route_kernel,
        out_shape=(jax.ShapeDtypeStruct((4, 4) + blk, bf), jax.ShapeDtypeStruct((2, 4, 4) + blk, bf),
                   jax.ShapeDtypeStruct(blk, bf), jax.ShapeDtypeStruct(blk, bf)),
        in_specs=[any_, any_],
        out_specs=(any_, any_, any_, any_),
        scratch_shapes=[pltpu.VMEM((2,) + blk, bf), pltpu.SemaphoreType.DMA((NCOPY,)),
                        pltpu.SemaphoreType.DMA((NCOPY,)), pltpu.SemaphoreType.DMA((4,))],
        compiler_params=pltpu.CompilerParams(collective_id=0, has_side_effects=True, vmem_limit_bytes=60 << 20),
        name="route",
    )(lq, rq)[:2]


AXES = ("grp_0", "grp_1", "grp_2", "sub")
K = 512
MAIN, PAIRED, TAIL, REM, TABLE = 0, 1536, 2304, 2400, 2528
PROWS = 1600


def pack(m, table):
    bf = jnp.bfloat16
    main = m[:, :192].reshape(16, 2, 4, 48, 200)
    x1 = main[..., :128].transpose(2, 1, 0, 3, 4).reshape(4, 1536, 128)
    x2 = main[..., 128:192].transpose(2, 0, 3, 1, 4).reshape(4, 768, 128)
    x3 = main[..., 192:].reshape(2, 8, 2, 4, 48, 8)
    x3 = x3[:, :, ::-1].transpose(3, 0, 4, 2, 1, 5).reshape(4, 96, 128)
    rem = jnp.pad(m[:, 192:], ((0, 0), (0, 0), (0, 56))).reshape(32, 4, 2, 2, 128)
    rem = rem.transpose(1, 3, 0, 2, 4).reshape(4, 128, 128)
    table = jnp.broadcast_to(table[None], (4, 16, 128))
    return jnp.concatenate([x1, x2, x3, rem, table], axis=1).astype(bf)


def slot_table(dimers, coupling):
    source = dimers[:, 0] // 32
    same = (source[:, None] == source[None, :]).astype(jnp.int32)
    count = source.shape[0]
    before = jnp.arange(count)[None, :] < jnp.arange(count)[:, None]
    rank = jnp.sum(jnp.where(before, same, 0), axis=1)
    scale = coupling * jnp.float32(2.0 / math.sqrt(200.0))
    hi = lax.reduce_precision(scale, 8, 7)
    mid = lax.reduce_precision(scale - hi, 8, 7)
    low = scale - hi - mid
    li = (dimers[:, 0] % 32).astype(jnp.float32)
    lj = (dimers[:, 1] % 32).astype(jnp.float32)
    one = jnp.ones_like(scale)
    zero = jnp.zeros_like(scale)
    fields = jnp.stack([li, lj, hi, mid, low, one, zero, zero]).astype(jnp.bfloat16)
    hot = source[:, None] == jnp.arange(128)[None, :]
    picks = jnp.stack([hot & (rank == 0)[:, None], hot & (rank == 1)[:, None]], axis=1)
    picks = picks.reshape(count, 256).astype(jnp.bfloat16)
    table = jnp.dot(fields, picks, preferred_element_type=jnp.float32)
    return table.astype(jnp.bfloat16).reshape(16, 128), source, rank


def weights(u):
    u = jnp.pad(u, ((0, 0), (0, K - 400)))
    a, b, t = u[:128], u[128:192], jnp.tile(u[192:], (8, 1))
    return jnp.stack([
        jnp.concatenate([a, b, t]),
        jnp.concatenate([a, t, b]),
        jnp.pad(u, ((0, 56), (0, 0))),
    ])


def meet_kernel(pos, slots, scales, l_ref, r_ref, u_ref, w_ref, um_ref, ur_ref, out_ref, p_ref, q_ref, dl_ref, lhs_ref):
    step = pl.program_id(0)

    def product(src, weight, store):
        lane = lax.broadcasted_iota(jnp.int32, (48, 128), 1)
        for e in range(2):
            own = (lane < 64) if e == 0 else (lane >= 64)
            lhs_ref[e * 768:(e + 1) * 768, :128] = src[e * 768:(e + 1) * 768, :]
            for p in range(16):
                tail = (lane // 8) == (p % 8 + (8 if e == 0 else 0))
                x2 = src[PAIRED + 48 * p:PAIRED + 48 * p + 48, :]
                x3 = src[TAIL + 48 * (p // 8):TAIL + 48 * (p // 8) + 48, :]
                second = jnp.where(own, x2, jnp.where(tail, x3, jnp.zeros_like(x3)))
                at = e * 768 + 48 * p
                lhs_ref[at:at + 48, 128:] = second
        for h in range(2):
            lhs_ref[1536:1600, 128 * h:128 * h + 128] = src[REM + 64 * h:REM + 64 * h + 64, :]
        for e in range(2):
            @pl.loop(0, 3)
            def _(t):
                rows = pl.ds(pl.multiple_of(e * 768 + 256 * t, 256), 256)
                store(rows, jnp.dot(lhs_ref[rows, :], weight[e], preferred_element_type=jnp.float32))
        rows = pl.ds(1536, 64)
        store(rows, jnp.dot(lhs_ref[rows, :], weight[2], preferred_element_type=jnp.float32))

    @pl.when(step < 16)
    def _():
        def store(rows, value):
            p_ref[step, rows, :] = value

        product(l_ref.at[0], u_ref, store)

        @pl.loop(0, 32)
        def _(f):
            at = pl.multiple_of((f & 1) * 768 + (f >> 1) * 48, 8)
            prod = p_ref[step, pl.ds(at, 48), :] * um_ref[...]
            total = jnp.sum(prod, axis=0, keepdims=True)
            for r in range(2):
                total += p_ref[step, pl.ds(1536 + 2 * f + r, 1), :] * ur_ref[r:r + 1, :]
            dl_ref[pl.ds(step * 32 + f, 1), :] = total

    @pl.when(step >= 16)
    def _():
        o = step - 16

        def store(rows, value):
            q_ref[rows, :] = value

        product(r_ref.at[0], w_ref, store)

        @pl.loop(0, 32)
        def _(n):
            word = slots[o * 32 + n]

            @pl.when(word >= 1024)
            def _():
                li, lj = word & 31, (word >> 5) & 31
                s = (((n >> 3) - pos[0]) & 3) * 4 + (((n >> 1) & 3) - pos[1] & 3)
                pi = pl.multiple_of((li & 1) * 768 + (li >> 1) * 48, 8)
                qj = pl.multiple_of((lj & 1) * 768 + (lj >> 1) * 48, 8)
                prod = p_ref[s, pl.ds(pi, 48), :] * q_ref[pl.ds(qj, 48), :]
                total = jnp.sum(prod, axis=0, keepdims=True)
                for r in range(2):
                    total += p_ref[s, pl.ds(1536 + 2 * li + r, 1), :] * q_ref[pl.ds(1536 + 2 * lj + r, 1), :]
                out_ref[0, pl.ds(n, 1), :] = total * scales[o * 32 + n] + dl_ref[pl.ds(s * 32 + li, 1), :]


def meet(pos, slots, scales, lg, rg, u, w, um, ur):
    blk = (1, ROWS, 128)
    whole = lambda a: pl.BlockSpec(a.shape, lambda i, *_: (0,) * a.ndim, pipeline_mode=pl.Buffered(1))
    return pl.pallas_call(
        meet_kernel,
        out_shape=jax.ShapeDtypeStruct((32, 32, K), jnp.float32),
        grid_spec=pltpu.PrefetchScalarGridSpec(
            num_scalar_prefetch=3, grid=(48,),
            in_specs=[
                pl.BlockSpec(blk, lambda i, *_: (jnp.minimum(i, 15), 0, 0)),
                pl.BlockSpec(blk, lambda i, *_: (jnp.maximum(i - 16, 0), 0, 0)),
                whole(u), whole(w), whole(um), whole(ur),
            ],
            out_specs=pl.BlockSpec((1, 32, K), lambda i, *_: (jnp.maximum(i - 16, 0), 0, 0)),
            scratch_shapes=[
                pltpu.VMEM((16, PROWS, K), jnp.float32), pltpu.VMEM((PROWS, K), jnp.float32),
                pltpu.VMEM((512, K), jnp.float32), pltpu.VMEM((PROWS, 256), jnp.bfloat16),
            ],
        ),
        compiler_params=pltpu.CompilerParams(dimension_semantics=("arbitrary",), vmem_limit_bytes=67043328),
        name="meet",
    )(pos, slots, scales, lg.reshape(16, ROWS, 128), rg.reshape(32, ROWS, 128), u, w, um, ur)


def finish_kernel(where, parts, dr_ref, en_ref, sum_ref, got_ref, part_ref, inbox_ref, send, recv, loc):
    z, y, x, c = (lax.axis_index(n) for n in AXES)

    def dev(dz=0, dy=0, dx=0, dc=0):
        return (lax.rem(z + dz, 4), lax.rem(y + dy, 4), lax.rem(x + dx, 4), lax.rem(c + dc, 2))

    barrier = pltpu.get_barrier_semaphore()
    plane = [(dc, dy, dx) for dx in (2, 1, 3, 0) for dy in (2, 1, 3, 0) for dc in (1, 0)][:-1]
    partners = [dev(dc=dc, dy=dy, dx=dx) for dc, dy, dx in plane] + [dev(dz=d) for d in (1, 2, 3)]
    for p in partners:
        pl.semaphore_signal(barrier, inc=1, device_id=p, device_id_type=MESH)
    pl.semaphore_wait(barrier, len(partners))
    copies = []

    def send_to(src, dst, to):
        i = len(copies)
        copy = pltpu.make_async_remote_copy(
            src_ref=src, dst_ref=dst, send_sem=send.at[i], recv_sem=recv.at[i],
            device_id=to, device_id_type=MESH)
        copy.start()
        copies.append(copy)
        return copy

    for dc, dy, dx in plane:
        send_to(parts.at[dc, dy, dx], got_ref.at[dc, (4 - dy) % 4, (4 - dx) % 4], dev(dc=dc, dy=dy, dx=dx))
    own = pltpu.make_async_copy(parts.at[0, 0, 0], got_ref.at[0, 0, 0], loc.at[0])
    own.start()
    own.wait()
    for copy in copies:
        copy.wait_recv()

    me = ((z * 4 + y) * 4 + x) * 2 + c

    @pl.loop(0, 128)
    def _(d):
        dc, dy, n, lj = where[0, d], where[1, d], where[2, d], where[3, d]
        row = dr_ref[pl.ds(lj, 1), :]
        for dx in range(4):
            row += got_ref[dc, dy, dx, pl.ds(n, 1), :]
        en_ref[pl.ds(d, 1), :] = row[:, :400]

    value = en_ref[...]
    mean = jnp.sum(value * value, axis=1, keepdims=True) * jnp.float32(1.0 / 400.0)
    index = (me * 128 + lax.broadcasted_iota(jnp.int32, (128, 1), 0)).astype(jnp.float32)
    total = jnp.sum((index + 1.0) * jnp.float32(1.0 / 16384.0) * mean, axis=0, keepdims=True)
    total = jnp.broadcast_to(total * jnp.float32(2.0 / 16384.0), (8, 128))
    stages = [[dict(dx=d) for d in (1, 2, 3)], [dict(dy=d) for d in (1, 2, 3)], [dict(dz=d) for d in (1, 2, 3)], [dict(dc=1)]]
    slot = 0
    for k, stage in enumerate(stages):
        part_ref[k] = total
        sent = []
        for j, to in enumerate(stage):
            sent.append((slot, send_to(part_ref.at[k], inbox_ref.at[slot], dev(**to))))
            slot += 1
        for at, copy in sent:
            copy.wait_recv()
        values = [total] + [inbox_ref[at] for at, _ in sent]
        if len(values) == 4:
            total = (values[0] + values[2]) + (values[1] + values[3])
        else:
            total = values[0] + values[1]
    sum_ref[...] = total
    for copy in copies:
        copy.wait_send()


def finish(where, parts, dr):
    n = 41
    vmem = pl.BlockSpec(memory_space=pltpu.VMEM)
    return pl.pallas_call(
        finish_kernel,
        out_shape=(jax.ShapeDtypeStruct((128, 400), jnp.float32), jax.ShapeDtypeStruct((8, 128), jnp.float32)),
        in_specs=[pl.BlockSpec(memory_space=pltpu.SMEM), pl.BlockSpec(memory_space=pl.ANY), vmem],
        out_specs=(vmem, vmem),
        scratch_shapes=[
            pltpu.VMEM((2, 4, 4, 32, K), jnp.float32), pltpu.VMEM((4, 8, 128), jnp.float32),
            pltpu.VMEM((10, 8, 128), jnp.float32), pltpu.SemaphoreType.DMA((n,)),
            pltpu.SemaphoreType.DMA((n,)), pltpu.SemaphoreType.DMA((1,)),
        ],
        compiler_params=pltpu.CompilerParams(collective_id=1, has_side_effects=True, vmem_limit_bytes=32 << 20),
        name="finish",
    )(where, parts.reshape(2, 4, 4, 32, K), dr)


def local(potentials, dimers, coupling, transform):
    z, y, x, c = (lax.axis_index(n) for n in AXES)
    upper, lower = transform[:200], transform[200:]
    table, source, rank = slot_table(dimers, coupling)
    lq = pack(potentials.transpose(0, 2, 1), jnp.zeros_like(table))
    rq = pack(potentials, table)
    lg, rg = route(lq, rq)

    tab = rg[:, :, :, TABLE:, :].reshape(32, 8, 2, 4, 4, 4, 2)
    tab = lax.dynamic_index_in_dim(tab, y, 4, keepdims=False)
    tab = lax.dynamic_index_in_dim(tab, c, 5, keepdims=False)
    tab = tab.transpose(1, 0, 3, 4, 2).reshape(8, 1024).astype(jnp.float32)
    slots = (tab[0] + 32.0 * tab[1] + 1024.0 * tab[5]).astype(jnp.int32)
    scales = tab[2] + tab[3] + tab[4]

    pad = ((0, 0), (0, K - 400))
    up = jnp.pad(upper, pad).astype(jnp.float32)
    um = lax.dynamic_slice_in_dim(up, 48 * x, 48, 0)
    ur = lax.dynamic_slice_in_dim(up, 192 + 2 * x, 2, 0)
    pos = jnp.stack([z, x])
    parts = meet(pos, slots, scales, lg, rg, weights(upper), weights(lower), um, ur)

    own = jnp.einsum("fab,bk->fak", potentials, lower, preferred_element_type=jnp.float32)
    dr = jnp.pad(jnp.sum(own * lower.astype(jnp.float32)[None], axis=1), pad)
    zs, ys, xs, cs = source // 32, (source // 8) % 4, (source // 2) % 4, source % 2
    where = jnp.stack([(cs - c) % 2, (ys - y) % 4, (zs * 4 + xs) * 2 + rank, dimers[:, 1] % 32])
    energies, total = finish(where, parts, dr)
    return energies, total[0, :1]


def solution(mesh):
    split = Mesh(mesh.devices.reshape(4, 4, 4, mesh.shape["sub"]), AXES)
    return jax.shard_map(
        local,
        mesh=split,
        in_specs=(P(AXES, None, None), P(AXES, None), P(AXES), P()),
        out_specs=(P(AXES, None), P()),
        check_vma=False,
    )
```

time: 639 us -> 360 us (0.56)
  Pallas kernels: 0 us -> 283 us
  waiting for transfers between devices: 245 us -> 0 us
  matrix products: 108 us -> 4.25 us
  blocking collectives: 66.9 us -> 0 us
  local copies, waits for them, and re-layouts: 119 us -> 61.3 us
  other arithmetic: 64.7 us -> 9.26 us
  starting transfers between devices: 29.9 us -> 0 us
    pallas_call x0 -> x3, Pallas kernels: none -> 283 us  [the longest x1 130 us: meet(): pl.pallas_call(meet_kernel, out_shape=jax.ShapeDtypeStruct((32, 32, K), j...]
    all_to_all x2 -> x0, waiting for transfers between devices: 245 us -> none  [several_exchanges(): lax.all_to_all(section, axis, split_axis=0, concat_axis=0, tiled=True)]
    dot_general x80 -> x2, matrix products: 108 us -> 4.25 us  [the longest x1 4.12 us: local(): jnp.einsum('fab,bk->fak', potentials, lower, preferred_element_type=jnp.f...]
    gather x4 -> x0, local copies, waits for them, and re-layouts: 56.3 us -> none  [the longest x2 35 us: local(): jnp.take(arrived.reshape(owners * cap, basis, basis), slots, axis=0)]
    psum x4 -> x0, blocking collectives: 45.9 us -> none  [over_axes(): value = lax.psum(value, axis)]
    split x3 -> x0, local copies, waits for them, and re-layouts: 41.9 us -> none  [several_exchanges(): jnp.split(tiles, edges_of(tiles.shape[widest], pieces), axis=widest)]
    select_n x5 -> x3, other arithmetic: 39.5 us -> 2.64 us  [the longest x1 1.31 us: local(): (cs - c) % 2]
    all_to_all x2 -> x0, starting transfers between devices: 29.9 us -> none  [several_exchanges(): lax.all_to_all(section, axis, split_axis=0, concat_axis=0, tiled=True)]
  transfers between devices with their start and end apart: 2 -> 0, of which waited for: 2 -> 0; matrix products, arithmetic and copies ran while one was open for 11% -> 0% of each run, Pallas kernels for 0% -> 0%
where the time goes in v1:
time: 360 us; the launch traced here: 359 us
  Pallas kernels  283 us (79%)
  local copies, waits for them, and re-layouts  61.3 us (17%)
  other arithmetic  9.26 us (3%)
  matrix products  4.25 us (1%)
    pallas_call x1, Pallas kernels, meet(): pl.pallas_call(meet_kernel, out_shape=jax.ShapeDtypeStruct((32, 32, K), j...  130 us
    pallas_call x1, Pallas kernels, route(): pl.pallas_call(route_kernel, out_shape=(jax.ShapeDtypeStruct((4, 4) + blk...  106 us
    pallas_call x1, Pallas kernels, finish(): pl.pallas_call(finish_kernel, out_shape=(jax.ShapeDtypeStruct((128, 400),...  47.7 us
    unnamed x16, local copies, waits for them, and re-layouts  17 us
    reshape x2, local copies, waits for them, and re-layouts, pack(): x2 = main[..., 128:192].transpose(2, 0, 3, 1, 4).reshape(4, 768, 128)  7.77 us

profile of v1, /device:TPU:1, one launch (start us, length us, event | category | flops | bytes accessed | tf_op | source)
XLA Modules:
  0.0 359.4 jit_solution(4156300545147104451)
XLA Ops:
  0.6 0.7 fusion.15
  1.3 1.3 and_select_fusion.10
  2.6 0.7 fusion.11
  3.3 0.7 fusion.21
  4.0 0.7 and_select_fusion.2
  4.9 0.5 copy-done.2
  5.6 5.7 %copy.66 = bf16[32,200,200]{1,2,0:T(8,128)(2,1)} copy(bf16[32,200,200]{2,1,0:T(8,128)(2,1)} %param.4) | data formatting | bytes 5120000 | tf_op args[0]
  11.3 2.1 slice.128
  13.4 0.3 slice_bitcast_fusion.3
  13.8 1.4 constant_dynamic-update-slice_fusion.4
  15.6 2.8 copy.68
  18.3 3.9 %reshape.694 = bf16[4,768,128]{2,1,0:T(8,128)(2,1)} reshape(bf16[4,16,48,2,64]{4,3,2,1,0:T(2,128)(2,1)} %copy.68) | data formatting | bytes 1572864 | tf_op jit(solution)/shard_map/reshape | solution.py:137
  22.2 2.2 constant_dynamic-update-slice_fusion.3
  24.4 1.7 slice.131
  26.1 1.7 copy.69
  28.4 0.7 constant_dynamic-update-slice_fusion.2
  29.0 0.9 slice.132
  30.1 0.7 constant_dynamic-update-slice_fusion.1
  30.8 2.1 slice.105
  32.9 0.3 slice_bitcast_fusion.1
  33.3 1.5 constant_dynamic-update-slice_fusion.9
  35.1 2.8 copy.74
  37.9 3.9 %reshape.701 = bf16[4,768,128]{2,1,0:T(8,128)(2,1)} reshape(bf16[4,16,48,2,64]{4,3,2,1,0:T(2,128)(2,1)} %copy.74) | data formatting | bytes 1572864 | tf_op jit(solution)/shard_map/reshape | solution.py:137
  41.8 2.2 constant_dynamic-update-slice_fusion.8
  43.9 1.7 slice.135
  45.6 1.9 copy.75
  48.1 0.7 constant_dynamic-update-slice_fusion.7
  49.0 0.7 constant_dynamic-update-slice_fusion.6
  49.7 0.6 constant_dynamic-update-slice_fusion
  50.3 106.1 %route.1 = (bf16[4,4,2544,128]{3,2,1,0:T(8,128)(2,1)}, bf16[2,4,4,2544,128]{4,3,2,1,0:T(8,128)(2,1)}, bf16[2544,128]{1,0:T(8,128)(2,1)}, bf16[2544,128]{1,0:T(8,128)(2,1)}) custom-call(bf16[4,2544,128]{2,1,0:T(8,128)(2,1)} %get-tuple-element.46.lq, bf16[4,2544,128]{2,1,0:T(8,128)(2,1)} %get-tuple-element.47.rq), custom_call_target="tpu_custom_call" | custom-call | tf_op jit(solution)/shard_map/route/pallas_call | solution.py:114
  156.4 0.9 slice.110
  157.3 3.6 %copy.79 = bf16[2,4,4,16,128]{2,1,0,4,3:T(4,128)(2,1)} copy(bf16[2,4,4,16,128]{4,3,2,1,0:T(8,128)(2,1)S(1)} %slice.110) | data formatting | bytes 262144 | tf_op jit(solution)/shard_map/slice | solution.py:361
  160.9 6.7 %reshape.707 = bf16[32,8,2,4,4,4,2]{0,6,5,4,3,2,1:T(2,128)(2,1)S(1)} reshape(bf16[2,4,4,16,128]{2,1,0,4,3:T(4,128)(2,1)} %copy.79) | data formatting | bytes 262144 | tf_op jit(solution)/shard_map/reshape | solution.py:361
  168.1 0.8 add.222.scales
  169.2 0.8 reshape.711.slots
  170.1 0.8 slice_convert_fusion
  171.1 1.0 pad_maximum_fusion.u_ref
  172.3 1.0 pad_maximum_fusion.1.w_ref
  173.3 0.7 constant_dynamic-slice_fusion.1.um_ref
  173.9 0.6 constant_dynamic-slice_fusion.ur_ref
  174.5 0.6 pad_add_fusion.2.pos
  175.2 129.7 %meet.1 = f32[32,32,512]{2,1,0:T(8,128)} custom-call(s32[2]{0:T(128)} %pad_add_fusion.2.pos, s32[1024]{0:T(1024)} %reshape.711.slots, f32[1024]{0:T(1024)} %add.222.scales, bf16[16,2544,128]{2,1,0:T(8,128)(2,1)} %bitcast.111, bf16[32,2544,128]{2,1,0:T(8,128)(2,1)} %bitcast.102, bf16[3,256,512]{2,1,0:T(8,128)(2,1)} %pad_maximum_fusion.u_ref, ...), custom_call_target="tpu_custom_call" | custom-call | tf_op jit(solution)/shard_map/meet/pallas_call | solution.py:248
  304.9 0.6 and_select_fusion.7
  305.6 0.7 pad_add_fusion.1.where
  306.3 4.1 %multiply_reduce_fusion = f32[32,400]{1,0:T(8,128)S(1)} fusion(bf16[32,200,200]{2,1,0:T(8,128)(2,1)} %param.4, f32[200,400]{1,0:T(8,128)} %get-tuple-element.26, bf16[400,400]{1,0:T(8,128)(2,1)} %param.7), kind=kOutput, calls=%fused_computation | convolution fusion | flops 1029107200 | bytes 3942400 | tf_op jit(solution)/shard_map/fab,bk->fak/dot_general | solution.py:375
  310.4 47.7 %finish.1 = (f32[128,400]{1,0:T(8,128)S(1)}, f32[8,128]{1,0:T(8,128)S(1)}) custom-call(s32[4,128]{1,0:T(4,128)S(1)} %pad_add_fusion.1.where, f32[2,4,4,32,512]{4,3,2,1,0:T(8,128)S(1)} %bitcast.101, f32[32,512]{1,0:T(8,128)S(1)} %pad.32.dr_ref), custom_call_target="tpu_custom_call" | custom-call | tf_op jit(solution)/shard_map/finish/pallas_call | solution.py:338
  358.1 0.8 copy.84
  358.9 0.5 slice.127
  (56 shorter events, 3.6 us)
Async XLA Ops:
  4.9 0.5 copy-start.2
  45.6 3.2 slice-start
  160.9 9.2 %copy-start.1 = (bf16[400,400]{1,0:T(8,128)(2,1)S(1)}, bf16[400,400]{1,0:T(8,128)(2,1)}, u32[]{:S(2)}) copy-start(bf16[400,400]{1,0:T(8,128)(2,1)} %param.7) | copy-start | bytes 960004
  306.3 4.1 %copy-start = (f32[32,32,512]{2,1,0:T(8,128)S(1)}, f32[32,32,512]{2,1,0:T(8,128)}, u32[]{:S(2)}) copy-start(f32[32,32,512]{2,1,0:T(8,128)} %meet.1) | copy-start | bytes 6291460

commit v2 on v1

--- a/solution.py
+++ b/solution.py
@@ -130,17 +130,67 @@
 PROWS = 1600
 
 
-def pack(m, table):
-    bf = jnp.bfloat16
-    main = m[:, :192].reshape(16, 2, 4, 48, 200)
-    x1 = main[..., :128].transpose(2, 1, 0, 3, 4).reshape(4, 1536, 128)
-    x2 = main[..., 128:192].transpose(2, 0, 3, 1, 4).reshape(4, 768, 128)
-    x3 = main[..., 192:].reshape(2, 8, 2, 4, 48, 8)
-    x3 = x3[:, :, ::-1].transpose(3, 0, 4, 2, 1, 5).reshape(4, 96, 128)
-    rem = jnp.pad(m[:, 192:], ((0, 0), (0, 0), (0, 56))).reshape(32, 4, 2, 2, 128)
-    rem = rem.transpose(1, 3, 0, 2, 4).reshape(4, 128, 128)
-    table = jnp.broadcast_to(table[None], (4, 16, 128))
-    return jnp.concatenate([x1, x2, x3, rem, table], axis=1).astype(bf)
+def pack_kernel(pot_ref, perm_ref, tab_ref, lq_ref, rq_ref, wide_ref, rem_ref):
+    lane = lax.broadcasted_iota(jnp.int32, (192, 128), 1)
+    zero = jnp.zeros((192, 128), jnp.float32)
+    wide_ref[...] = jnp.zeros_like(wide_ref)
+    outs = (lq_ref, rq_ref)
+
+    def pair(g, p, tails):
+        new = []
+        for side in range(2):
+            out = outs[side]
+            for e in range(2):
+                f = 16 * g + 2 * p + e
+                m = pot_ref[f].astype(jnp.float32)
+                if side == 0:
+                    m = m.T
+                wide_ref[side, e, :, :200] = m
+                rem_ref[side, pl.ds(pl.multiple_of(8 * f, 8), 8), :] = wide_ref[side, e, 192:200, :]
+                for q in range(4):
+                    at = pl.multiple_of(e * 768 + 48 * (8 * g + p), 16)
+                    out[q, pl.ds(at, 48), :] = m[48 * q:48 * q + 48, :128].astype(jnp.bfloat16)
+            s0 = wide_ref[side, 0, :192, 128:]
+            s1 = wide_ref[side, 1, :192, 128:]
+            x2 = jnp.where(lane < 64, s0, pltpu.roll(s1, 64, 1)).astype(jnp.bfloat16)
+            for q in range(4):
+                at = pl.multiple_of(PAIRED + 48 * (8 * g + p), 16)
+                out[q, pl.ds(at, 48), :] = x2[48 * q:48 * q + 48]
+            block = lane // 8
+            tail = jnp.where(block == 8 + p, pltpu.roll(s0, 8 * p, 1), tails[side])
+            new.append(jnp.where(block == p, pltpu.roll(s1, 64 + 8 * p, 1), tail))
+        return tuple(new)
+
+    for g in range(2):
+        tails = lax.fori_loop(0, 8, functools.partial(pair, g), (zero, zero))
+        for side in range(2):
+            tail = tails[side].astype(jnp.bfloat16)
+            for q in range(4):
+                outs[side][q, TAIL + 48 * g:TAIL + 48 * g + 48, :] = tail[48 * q:48 * q + 48]
+    for side in range(2):
+        rem = jnp.dot(perm_ref[...], rem_ref[side].astype(jnp.bfloat16), preferred_element_type=jnp.float32)
+        for q in range(4):
+            for h in range(2):
+                at = REM + 64 * h
+                outs[side][q, at:at + 64, :] = rem[64 * q:64 * q + 64, 128 * h:128 * h + 128].astype(jnp.bfloat16)
+            outs[side][q, TABLE:, :] = tab_ref[...]
+
+
+def pack(potentials, table):
+    row = jnp.arange(256)
+    q, f, r = row // 64, (row % 64) // 2, row % 2
+    perm = ((f * 8 + 2 * q + r)[:, None] == row[None, :]).astype(jnp.bfloat16)
+    vmem = pl.BlockSpec(memory_space=pltpu.VMEM)
+    shape = jax.ShapeDtypeStruct((4, ROWS, 128), jnp.bfloat16)
+    return pl.pallas_call(
+        pack_kernel,
+        out_shape=(shape, shape),
+        in_specs=[vmem, vmem, vmem],
+        out_specs=(vmem, vmem),
+        scratch_shapes=[pltpu.VMEM((2, 2, 200, 256), jnp.float32), pltpu.VMEM((2, 256, 256), jnp.float32)],
+        compiler_params=pltpu.CompilerParams(vmem_limit_bytes=40 << 20),
+        name="pack",
+    )(potentials, perm, table)
 
 
 def slot_table(dimers, coupling):
@@ -171,110 +221,147 @@
     return jnp.stack([
         jnp.concatenate([a, b, t]),
         jnp.concatenate([a, t, b]),
-        jnp.pad(u, ((0, 56), (0, 0))),
     ])
 
 
-def meet_kernel(pos, slots, scales, l_ref, r_ref, u_ref, w_ref, um_ref, ur_ref, out_ref, p_ref, q_ref, dl_ref, lhs_ref):
+def meet_kernel(gi_ref, gj_ref, li_ref, lj_ref, scales, l_ref, r_ref, u_ref, w_ref, um_ref, ur_ref, got_ref, p_ref, pr_ref, q_ref, qr_ref, dl_ref, lhs_ref, out_ref, send, recv, loc):
     step = pl.program_id(0)
-
-    def product(src, weight, store):
+    z, y, x, c = (lax.axis_index(n) for n in AXES)
+
+    def dev(o):
+        return (z, lax.rem(y + lax.rem(o // 4, 4), 4), lax.rem(x + lax.rem(o, 4), 4), lax.rem(c + o // 16, 2))
+
+    def copy_of(o):
+        to = (o // 16) * 16 + lax.rem(4 - lax.rem(o // 4, 4), 4) * 4 + lax.rem(4 - lax.rem(o, 4), 4)
+        return pltpu.make_async_remote_copy(
+            src_ref=out_ref.at[o], dst_ref=got_ref.at[to], send_sem=send.at[o], recv_sem=recv.at[o],
+            device_id=dev(o), device_id_type=MESH)
+
+    @pl.when(step == 0)
+    def _():
+        barrier = pltpu.get_barrier_semaphore()
+        for o in range(1, 32):
+            pl.semaphore_signal(barrier, inc=1, device_id=dev(jnp.int32(o)), device_id_type=MESH)
+        pl.semaphore_wait(barrier, 31)
+
+    def product(src, weight, store, rest):
         lane = lax.broadcasted_iota(jnp.int32, (48, 128), 1)
         for e in range(2):
             own = (lane < 64) if e == 0 else (lane >= 64)
-            lhs_ref[e * 768:(e + 1) * 768, :128] = src[e * 768:(e + 1) * 768, :]
+            lhs_ref[e * 832:e * 832 + 768, :128] = src[e * 768:(e + 1) * 768, :]
             for p in range(16):
                 tail = (lane // 8) == (p % 8 + (8 if e == 0 else 0))
                 x2 = src[PAIRED + 48 * p:PAIRED + 48 * p + 48, :]
                 x3 = src[TAIL + 48 * (p // 8):TAIL + 48 * (p // 8) + 48, :]
                 second = jnp.where(own, x2, jnp.where(tail, x3, jnp.zeros_like(x3)))
-                at = e * 768 + 48 * p
+                at = e * 832 + 48 * p
                 lhs_ref[at:at + 48, 128:] = second
         for h in range(2):
-            lhs_ref[1536:1600, 128 * h:128 * h + 128] = src[REM + 64 * h:REM + 64 * h + 64, :]
-        for e in range(2):
-            @pl.loop(0, 3)
-            def _(t):
-                rows = pl.ds(pl.multiple_of(e * 768 + 256 * t, 256), 256)
-                store(rows, jnp.dot(lhs_ref[rows, :], weight[e], preferred_element_type=jnp.float32))
-        rows = pl.ds(1536, 64)
-        store(rows, jnp.dot(lhs_ref[rows, :], weight[2], preferred_element_type=jnp.float32))
+            lhs_ref[768:832, 128 * h:128 * h + 128] = src[REM + 64 * h:REM + 64 * h + 64, :]
+        first = jnp.dot(lhs_ref[:832, :], weight[0], preferred_element_type=jnp.float32)
+        store(0, first[:768].reshape(48, 16, K))
+        rest(first[768:])
+        second = jnp.dot(lhs_ref[832:, :], weight[1], preferred_element_type=jnp.float32)
+        store(48, second.reshape(48, 16, K))
 
     @pl.when(step < 16)
     def _():
-        def store(rows, value):
-            p_ref[step, rows, :] = value
-
-        product(l_ref.at[0], u_ref, store)
-
-        @pl.loop(0, 32)
-        def _(f):
-            at = pl.multiple_of((f & 1) * 768 + (f >> 1) * 48, 8)
-            prod = p_ref[step, pl.ds(at, 48), :] * um_ref[...]
-            total = jnp.sum(prod, axis=0, keepdims=True)
-            for r in range(2):
-                total += p_ref[step, pl.ds(1536 + 2 * f + r, 1), :] * ur_ref[r:r + 1, :]
-            dl_ref[pl.ds(step * 32 + f, 1), :] = total
+        def store(at, value):
+            p_ref[step, at:at + 48] = value
+
+        def rest(value):
+            pr_ref[step] = value
+
+        product(l_ref.at[0], u_ref, store, rest)
+
+        @pl.loop(0, 8)
+        def _(t):
+            for k in range(4):
+                f = 4 * t + k
+                group = (k % 2) * 48 + (2 * t + k // 2) * 3
+                prod = p_ref[step, pl.ds(group, 3)].reshape(48, K) * um_ref[...]
+                total = jnp.sum(prod, axis=0, keepdims=True)
+                for r in range(2):
+                    total += pr_ref[step, pl.ds(2 * f + r, 1), :] * ur_ref[r:r + 1, :]
+                dl_ref[step, pl.ds(f, 1), :] = total
 
     @pl.when(step >= 16)
     def _():
-        o = step - 16
-
-        def store(rows, value):
-            q_ref[rows, :] = value
-
-        product(r_ref.at[0], w_ref, store)
-
-        @pl.loop(0, 32)
-        def _(n):
-            word = slots[o * 32 + n]
-
-            @pl.when(word >= 1024)
-            def _():
-                li, lj = word & 31, (word >> 5) & 31
-                s = (((n >> 3) - pos[0]) & 3) * 4 + (((n >> 1) & 3) - pos[1] & 3)
-                pi = pl.multiple_of((li & 1) * 768 + (li >> 1) * 48, 8)
-                qj = pl.multiple_of((lj & 1) * 768 + (lj >> 1) * 48, 8)
-                prod = p_ref[s, pl.ds(pi, 48), :] * q_ref[pl.ds(qj, 48), :]
-                total = jnp.sum(prod, axis=0, keepdims=True)
-                for r in range(2):
-                    total += p_ref[s, pl.ds(1536 + 2 * li + r, 1), :] * q_ref[pl.ds(1536 + 2 * lj + r, 1), :]
-                out_ref[0, pl.ds(n, 1), :] = total * scales[o * 32 + n] + dl_ref[pl.ds(s * 32 + li, 1), :]
-
-
-def meet(pos, slots, scales, lg, rg, u, w, um, ur):
+        o = 47 - step
+
+        def store(at, value):
+            q_ref[at:at + 48] = value
+
+        def rest(value):
+            qr_ref[...] = value
+
+        product(r_ref.at[0], w_ref, store, rest)
+
+        @pl.loop(0, 8)
+        def _(t):
+            for k in range(4):
+                zs, xs, r = t // 2, lax.rem(t, 2) * 2 + k // 2, k % 2
+                lane = ((zs * 4 + y) * 4 + xs) * 2 + c
+                row = o * 2 + r
+                gi, gj, li, lj = gi_ref[row, lane], gj_ref[row, lane], li_ref[row, lane], lj_ref[row, lane]
+                s = lax.rem(zs - z + 4, 4) * 4 + lax.rem(xs - x + 4, 4)
+                prod = p_ref[s, pl.ds(gi, 3)] * q_ref[pl.ds(gj, 3)]
+                total = jnp.sum(prod.reshape(48, K), axis=0, keepdims=True)
+                for i in range(2):
+                    total += pr_ref[s, pl.ds(2 * li + i, 1), :] * qr_ref[pl.ds(2 * lj + i, 1), :]
+                out_ref[o, pl.ds(4 * t + k, 1), :] = total * scales[row, lane] + dl_ref[s, pl.ds(li, 1), :]
+
+        @pl.when(o > 0)
+        def _():
+            copy_of(o).start()
+
+        @pl.when(o == 0)
+        def _():
+            own = pltpu.make_async_copy(out_ref.at[0], got_ref.at[0], loc.at[0])
+            own.start()
+            own.wait()
+            for k in range(1, 32):
+                copy_of(jnp.int32(k)).wait_recv()
+            for k in range(1, 32):
+                copy_of(jnp.int32(k)).wait_send()
+
+
+def meet(tables, lg, rg, u, w, um, ur):
     blk = (1, ROWS, 128)
     whole = lambda a: pl.BlockSpec(a.shape, lambda i, *_: (0,) * a.ndim, pipeline_mode=pl.Buffered(1))
     return pl.pallas_call(
         meet_kernel,
         out_shape=jax.ShapeDtypeStruct((32, 32, K), jnp.float32),
         grid_spec=pltpu.PrefetchScalarGridSpec(
-            num_scalar_prefetch=3, grid=(48,),
+            num_scalar_prefetch=5, grid=(48,),
             in_specs=[
                 pl.BlockSpec(blk, lambda i, *_: (jnp.minimum(i, 15), 0, 0)),
-                pl.BlockSpec(blk, lambda i, *_: (jnp.maximum(i - 16, 0), 0, 0)),
+                pl.BlockSpec(blk, lambda i, *_: (jnp.minimum(47 - i, 31), 0, 0)),
                 whole(u), whole(w), whole(um), whole(ur),
             ],
-            out_specs=pl.BlockSpec((1, 32, K), lambda i, *_: (jnp.maximum(i - 16, 0), 0, 0)),
+            out_specs=pl.BlockSpec(memory_space=pl.ANY),
             scratch_shapes=[
-                pltpu.VMEM((16, PROWS, K), jnp.float32), pltpu.VMEM((PROWS, K), jnp.float32),
-                pltpu.VMEM((512, K), jnp.float32), pltpu.VMEM((PROWS, 256), jnp.bfloat16),
+                pltpu.VMEM((16, 96, 16, K), jnp.float32), pltpu.VMEM((16, 64, K), jnp.float32),
+                pltpu.VMEM((96, 16, K), jnp.float32), pltpu.VMEM((64, K), jnp.float32),
+                pltpu.VMEM((16, 32, K), jnp.float32), pltpu.VMEM((PROWS, 256), jnp.bfloat16),
+                pltpu.VMEM((32, 32, K), jnp.float32), pltpu.SemaphoreType.DMA((32,)),
+                pltpu.SemaphoreType.DMA((32,)), pltpu.SemaphoreType.DMA((1,)),
             ],
         ),
-        compiler_params=pltpu.CompilerParams(dimension_semantics=("arbitrary",), vmem_limit_bytes=67043328),
+        compiler_params=pltpu.CompilerParams(dimension_semantics=("arbitrary",), vmem_limit_bytes=67043328,
+                                             collective_id=2, has_side_effects=True),
         name="meet",
-    )(pos, slots, scales, lg.reshape(16, ROWS, 128), rg.reshape(32, ROWS, 128), u, w, um, ur)
-
-
-def finish_kernel(where, parts, dr_ref, en_ref, sum_ref, got_ref, part_ref, inbox_ref, send, recv, loc):
+    )(*tables, lg.reshape(16, ROWS, 128), rg.reshape(32, ROWS, 128), u, w, um, ur)
+
+
+def finish_kernel(where, got_ref, dr_ref, en_ref, sum_ref, part_ref, inbox_ref, send, recv):
     z, y, x, c = (lax.axis_index(n) for n in AXES)
 
     def dev(dz=0, dy=0, dx=0, dc=0):
         return (lax.rem(z + dz, 4), lax.rem(y + dy, 4), lax.rem(x + dx, 4), lax.rem(c + dc, 2))
 
     barrier = pltpu.get_barrier_semaphore()
-    plane = [(dc, dy, dx) for dx in (2, 1, 3, 0) for dy in (2, 1, 3, 0) for dc in (1, 0)][:-1]
-    partners = [dev(dc=dc, dy=dy, dx=dx) for dc, dy, dx in plane] + [dev(dz=d) for d in (1, 2, 3)]
+    partners = [dev(**{k: d}) for k in ("dx", "dy", "dz") for d in (1, 2, 3)] + [dev(dc=1)]
     for p in partners:
         pl.semaphore_signal(barrier, inc=1, device_id=p, device_id_type=MESH)
     pl.semaphore_wait(barrier, len(partners))
@@ -288,14 +375,6 @@
         copy.start()
         copies.append(copy)
         return copy
-
-    for dc, dy, dx in plane:
-        send_to(parts.at[dc, dy, dx], got_ref.at[dc, (4 - dy) % 4, (4 - dx) % 4], dev(dc=dc, dy=dy, dx=dx))
-    own = pltpu.make_async_copy(parts.at[0, 0, 0], got_ref.at[0, 0, 0], loc.at[0])
-    own.start()
-    own.wait()
-    for copy in copies:
-        copy.wait_recv()
 
     me = ((z * 4 + y) * 4 + x) * 2 + c
 
@@ -333,17 +412,17 @@
 
 
 def finish(where, parts, dr):
-    n = 41
+    n = 10
     vmem = pl.BlockSpec(memory_space=pltpu.VMEM)
     return pl.pallas_call(
         finish_kernel,
         out_shape=(jax.ShapeDtypeStruct((128, 400), jnp.float32), jax.ShapeDtypeStruct((8, 128), jnp.float32)),
-        in_specs=[pl.BlockSpec(memory_space=pltpu.SMEM), pl.BlockSpec(memory_space=pl.ANY), vmem],
+        in_specs=[pl.BlockSpec(memory_space=pltpu.SMEM), vmem, vmem],
         out_specs=(vmem, vmem),
         scratch_shapes=[
-            pltpu.VMEM((2, 4, 4, 32, K), jnp.float32), pltpu.VMEM((4, 8, 128), jnp.float32),
+            pltpu.VMEM((4, 8, 128), jnp.float32),
             pltpu.VMEM((10, 8, 128), jnp.float32), pltpu.SemaphoreType.DMA((n,)),
-            pltpu.SemaphoreType.DMA((n,)), pltpu.SemaphoreType.DMA((1,)),
+            pltpu.SemaphoreType.DMA((n,)),
         ],
         compiler_params=pltpu.CompilerParams(collective_id=1, has_side_effects=True, vmem_limit_bytes=32 << 20),
         name="finish",
@@ -354,23 +433,19 @@
     z, y, x, c = (lax.axis_index(n) for n in AXES)
     upper, lower = transform[:200], transform[200:]
     table, source, rank = slot_table(dimers, coupling)
-    lq = pack(potentials.transpose(0, 2, 1), jnp.zeros_like(table))
-    rq = pack(potentials, table)
+    lq, rq = pack(potentials, table)
     lg, rg = route(lq, rq)
 
-    tab = rg[:, :, :, TABLE:, :].reshape(32, 8, 2, 4, 4, 4, 2)
-    tab = lax.dynamic_index_in_dim(tab, y, 4, keepdims=False)
-    tab = lax.dynamic_index_in_dim(tab, c, 5, keepdims=False)
-    tab = tab.transpose(1, 0, 3, 4, 2).reshape(8, 1024).astype(jnp.float32)
-    slots = (tab[0] + 32.0 * tab[1] + 1024.0 * tab[5]).astype(jnp.int32)
-    scales = tab[2] + tab[3] + tab[4]
+    tab = rg[:, :, :, TABLE:, :].reshape(32, 16, 128).astype(jnp.float32)
+    li, lj = tab[:, 0:2].astype(jnp.int32).reshape(64, 128), tab[:, 2:4].astype(jnp.int32).reshape(64, 128)
+    scales = (tab[:, 4:6] + tab[:, 6:8] + tab[:, 8:10]).reshape(64, 128)
+    tables = [(v % 2) * 48 + (v // 2) * 3 for v in (li, lj)] + [li, lj, scales]
 
     pad = ((0, 0), (0, K - 400))
     up = jnp.pad(upper, pad).astype(jnp.float32)
     um = lax.dynamic_slice_in_dim(up, 48 * x, 48, 0)
     ur = lax.dynamic_slice_in_dim(up, 192 + 2 * x, 2, 0)
-    pos = jnp.stack([z, x])
-    parts = meet(pos, slots, scales, lg, rg, weights(upper), weights(lower), um, ur)
+    parts = meet(tables, lg, rg, weights(upper), weights(lower), um, ur)
 
     own = jnp.einsum("fab,bk->fak", potentials, lower, preferred_element_type=jnp.float32)
     dr = jnp.pad(jnp.sum(own * lower.astype(jnp.float32)[None], axis=1), pad)

time: 360 us -> 228 us (0.63)
  Pallas kernels: 283 us -> 206 us
  local copies, waits for them, and re-layouts: 61.3 us -> 8.55 us
    pallas_call x1, Pallas kernels: 130 us -> 77.5 us  [meet(): pl.pallas_call(meet_kernel, out_shape=jax.ShapeDtypeStruct((32, 32, K), j...]
    pallas_call x1, Pallas kernels: 47.7 us -> 16.2 us  [finish(): pl.pallas_call(finish_kernel, out_shape=(jax.ShapeDtypeStruct((128, 400),...]
    slice x11 -> x1, local copies, waits for them, and re-layouts: 16.7 us -> 0.92 us  [local(): tab = rg[:, :, :, TABLE:, :].reshape(32, 16, 128).astype(jnp.float32)]
    reshape x10 -> x1, local copies, waits for them, and re-layouts: 15.1 us -> 0.02 us  [slot_table(): return (table.astype(jnp.bfloat16).reshape(16, 128), source, rank)]
    unnamed x16 -> x17, local copies, waits for them, and re-layouts: 17 us -> 5.69 us
    transpose x13 -> x0, local copies, waits for them, and re-layouts: 7.56 us -> none  [the longest x4 6.13 us: pack(): x2 = main[..., 128:192].transpose(2, 0, 3, 1, 4).reshape(4, 768, 128)]
    pallas_call x0 -> x1, Pallas kernels: none -> 5.79 us  [pack(): pl.pallas_call(pack_kernel, out_shape=(shape, shape), in_specs=[vmem, vme...]
where the time goes in v2:
time: 228 us
  Pallas kernels  206 us (90%)
  local copies, waits for them, and re-layouts  8.55 us (4%)
  other arithmetic  8.49 us (4%)
  matrix products  4.24 us (2%)
    pallas_call x1, Pallas kernels, route(): pl.pallas_call(route_kernel, out_shape=(jax.ShapeDtypeStruct((4, 4) + blk...  106 us
    pallas_call x1, Pallas kernels, meet(): pl.pallas_call(meet_kernel, out_shape=jax.ShapeDtypeStruct((32, 32, K), j...  77.5 us
    pallas_call x1, Pallas kernels, finish(): pl.pallas_call(finish_kernel, out_shape=(jax.ShapeDtypeStruct((128, 400),...  16.2 us
    pallas_call x1, Pallas kernels, pack(): pl.pallas_call(pack_kernel, out_shape=(shape, shape), in_specs=[vmem, vme...  5.79 us
    unnamed x17, local copies, waits for them, and re-layouts  5.69 us

profile of v2, /device:TPU:1, one launch (start us, length us, event | category | flops | bytes accessed | tf_op | source)
XLA Modules:
  0.0 227.7 jit_solution(10550087937253742559)
XLA Ops:
  0.6 0.7 fusion.31
  1.3 0.8 and_select_fusion.14
  2.1 0.7 and_select_fusion.6
  2.8 0.7 fusion.37
  3.5 0.2 select_reduce_fusion
  3.7 0.6 pad_add_fusion.1.where
  4.3 0.1 fusion.perm_ref
  4.4 0.7 fusion.27
  5.2 0.1 convolution_convert_fusion
  5.3 0.0 copy-start.1
  5.4 1.9 copy-done.1
  7.3 5.8 %pack.1 = (bf16[4,2544,128]{2,1,0:T(8,128)(2,1)S(1)}, bf16[4,2544,128]{2,1,0:T(8,128)(2,1)S(1)}) custom-call(bf16[32,200,200]{2,1,0:T(8,128)(2,1)S(1)} %copy-done.1, bf16[256,256]{1,0:T(8,128)(2,1)S(1)} %fusion.perm_ref, bf16[16,128]{1,0:T(8,128)(2,1)S(1)} %reshape.678.tab_ref), custom_call_target="tpu_custom_call" | custom-call | tf_op jit(solution)/shard_map/pack/pallas_call | solution.py:185
  13.1 0.0 copy-start.2
  13.1 1.5 copy-done.2
  14.6 0.0 copy-start.3
  14.6 1.5 copy-done.3
  16.0 0.0 copy-start.5
  16.0 106.1 %route.1 = (bf16[4,4,2544,128]{3,2,1,0:T(8,128)(2,1)}, bf16[2,4,4,2544,128]{4,3,2,1,0:T(8,128)(2,1)}, bf16[2544,128]{1,0:T(8,128)(2,1)}, bf16[2544,128]{1,0:T(8,128)(2,1)}) custom-call(bf16[4,2544,128]{2,1,0:T(8,128)(2,1)} %copy-done.2, bf16[4,2544,128]{2,1,0:T(8,128)(2,1)} %copy-done.3), custom_call_target="tpu_custom_call" | custom-call | tf_op jit(solution)/shard_map/route/pallas_call | solution.py:114
  122.1 0.9 slice.61
  123.1 0.7 slice_add_fusion
  123.7 0.0 copy-start.6
  123.7 0.0 copy-start.7
  123.7 0.7 fusion.5
  124.4 0.0 copy-done.5
  124.4 0.8 slice_convert_fusion.2
  125.4 0.0 copy-done.6
  125.4 0.0 copy-done.7
  125.4 0.9 pad_maximum_fusion.u_ref
  126.3 0.9 pad_maximum_fusion.1.w_ref
  127.3 0.7 constant_dynamic-slice_fusion.1.um_ref
  127.9 0.6 constant_dynamic-slice_fusion.ur_ref
  128.5 77.5 %meet.1 = f32[32,32,512]{2,1,0:T(8,128)} custom-call(s32[64,128]{1,0:T(8,128)} %get-tuple-element.55.gi_ref, s32[64,128]{1,0:T(8,128)} %get-tuple-element.56.gj_ref, s32[64,128]{1,0:T(8,128)} %bitcast.69, s32[64,128]{1,0:T(8,128)} %bitcast.67, f32[64,128]{1,0:T(8,128)} %bitcast.70, bf16[16,2544,128]{2,1,0:T(8,128)(2,1)} %bitcast.65, ...), custom_call_target="tpu_custom_call" | custom-call | tf_op jit(solution)/shard_map/meet/pallas_call | solution.py:332
  206.0 0.0 copy-start
  206.0 0.0 copy-start.4
  206.0 4.1 %multiply_reduce_fusion = f32[32,400]{1,0:T(8,128)S(1)} fusion(bf16[32,200,200]{2,1,0:T(8,128)(2,1)} %pot_ref.1, f32[200,400]{1,0:T(8,128)} %get-tuple-element.26, bf16[400,400]{1,0:T(8,128)(2,1)} %param.7), kind=kOutput, calls=%fused_computation | convolution fusion | flops 1029107200 | bytes 3942400 | tf_op jit(solution)/shard_map/fab,bk->fak/dot_general | solution.py:450
  210.1 0.0 copy-done
  210.1 0.0 copy-done.4
  210.1 16.2 %finish.1 = (f32[128,400]{1,0:T(8,128)S(1)}, f32[8,128]{1,0:T(8,128)S(1)}) custom-call(s32[4,128]{1,0:T(4,128)S(1)} %copy-done.4, f32[2,4,4,32,512]{4,3,2,1,0:T(8,128)S(1)} %bitcast.63, f32[32,512]{1,0:T(8,128)S(1)} %pad.14.dr_ref), custom_call_target="tpu_custom_call" | custom-call | tf_op jit(solution)/shard_map/finish/pallas_call | solution.py:417
  226.3 0.8 copy.8
  227.2 0.5 slice.77
  (20 shorter events, 0.4 us)
Async XLA Ops:
  5.3 1.9 copy-start.1
  13.1 1.5 copy-start.2
  14.6 1.5 copy-start.3
  16.0 108.4 %copy-start.5 = (bf16[400,400]{1,0:T(8,128)(2,1)S(1)}, bf16[400,400]{1,0:T(8,128)(2,1)}, u32[]{:S(2)}) copy-start(bf16[400,400]{1,0:T(8,128)(2,1)} %param.7) | copy-start | bytes 960004
  123.7 1.6 copy-start.6
  123.7 1.6 copy-start.7
  206.0 4.2 %copy-start = (f32[32,32,512]{2,1,0:T(8,128)S(1)}, f32[32,32,512]{2,1,0:T(8,128)}, u32[]{:S(2)}) copy-start(f32[32,32,512]{2,1,0:T(8,128)} %meet.1) | copy-start | bytes 6291460
  206.0 4.2 %copy-start.4 = (s32[4,128]{1,0:T(4,128)S(1)}, s32[4,128]{1,0:T(4,128)}, u32[]{:S(2)}) copy-start(s32[4,128]{1,0:T(4,128)} %pad_add_fusion.1.where) | copy-start | bytes 6148

commit v3 on v2

v3 whole, which is shorter than its diff:
```python
import functools
import math
import jax
import jax.numpy as jnp
from jax import lax
from jax.experimental import pallas as pl
from jax.experimental.pallas import tpu as pltpu
from jax.sharding import Mesh
from jax.sharding import PartitionSpec as P

MESH = pl.DeviceIdType.MESH
AXES = ("grp_0", "grp_1", "grp_2", "sub")
K = 512
ROWS = 2528
HALF = 1280
NCOPY = 56
PAIRED, TAIL, REM = 1536, 2304, 2400
ORDER = {0: 0, 3: 1, 1: 2, 2: 3}


def pack_kernel(pot_ref, perm_ref, lq_ref, rq_ref, wide_ref, rem_ref):
    lane = lax.broadcasted_iota(jnp.int32, (192, 128), 1)
    zero = jnp.zeros((192, 128), jnp.float32)
    wide_ref[...] = jnp.zeros_like(wide_ref)
    outs = (lq_ref, rq_ref)

    def pair(g, p, tails):
        new = []
        for side in range(2):
            out = outs[side]
            for e in range(2):
                f = 16 * g + 2 * p + e
                m = pot_ref[f].astype(jnp.float32)
                if side == 0:
                    m = m.T
                wide_ref[side, e, :, :200] = m
                rem_ref[side, pl.ds(pl.multiple_of(8 * f, 8), 8), :] = wide_ref[side, e, 192:200, :]
                for q in range(4):
                    at = pl.multiple_of(e * 768 + 48 * (8 * g + p), 16)
                    out[q, pl.ds(at, 48), :] = m[48 * q:48 * q + 48, :128].astype(jnp.bfloat16)
            s0 = wide_ref[side, 0, :192, 128:]
            s1 = wide_ref[side, 1, :192, 128:]
            x2 = jnp.where(lane < 64, s0, pltpu.roll(s1, 64, 1)).astype(jnp.bfloat16)
            for q in range(4):
                at = pl.multiple_of(PAIRED + 48 * (8 * g + p), 16)
                out[q, pl.ds(at, 48), :] = x2[48 * q:48 * q + 48]
            block = lane // 8
            tail = jnp.where(block == 8 + p, pltpu.roll(s0, 8 * p, 1), tails[side])
            new.append(jnp.where(block == p, pltpu.roll(s1, 64 + 8 * p, 1), tail))
        return tuple(new)

    for g in range(2):
        tails = lax.fori_loop(0, 8, functools.partial(pair, g), (zero, zero))
        for side in range(2):
            tail = tails[side].astype(jnp.bfloat16)
            for q in range(4):
                outs[side][q, TAIL + 48 * g:TAIL + 48 * g + 48, :] = tail[48 * q:48 * q + 48]
    for side in range(2):
        rem = jnp.dot(perm_ref[...], rem_ref[side].astype(jnp.bfloat16), preferred_element_type=jnp.float32)
        for q in range(4):
            for h in range(2):
                at = REM + 64 * h
                outs[side][q, at:at + 64, :] = rem[64 * q:64 * q + 64, 128 * h:128 * h + 128].astype(jnp.bfloat16)


def pack(potentials):
    row = jnp.arange(256)
    q, f, r = row // 64, (row % 64) // 2, row % 2
    perm = ((f * 8 + 2 * q + r)[:, None] == row[None, :]).astype(jnp.bfloat16)
    vmem = pl.BlockSpec(memory_space=pltpu.VMEM)
    shape = jax.ShapeDtypeStruct((4, ROWS, 128), jnp.bfloat16)
    return pl.pallas_call(
        pack_kernel,
        out_shape=(shape, shape),
        in_specs=[vmem, vmem],
        out_specs=(vmem, vmem),
        scratch_shapes=[pltpu.VMEM((2, 2, 200, 256), jnp.float32), pltpu.VMEM((2, 256, 256), jnp.float32)],
        compiler_params=pltpu.CompilerParams(vmem_limit_bytes=40 << 20),
        name="pack",
    )(potentials, perm)


def slot_table(dimers, coupling):
    source = dimers[:, 0] // 32
    same = (source[:, None] == source[None, :]).astype(jnp.int32)
    count = source.shape[0]
    before = jnp.arange(count)[None, :] < jnp.arange(count)[:, None]
    rank = jnp.sum(jnp.where(before, same, 0), axis=1)
    scale = coupling * jnp.float32(2.0 / math.sqrt(200.0))
    hi = lax.reduce_precision(scale, 8, 7)
    mid = lax.reduce_precision(scale - hi, 8, 7)
    low = scale - hi - mid
    li = (dimers[:, 0] % 32).astype(jnp.float32)
    lj = (dimers[:, 1] % 32).astype(jnp.float32)
    zero = jnp.zeros_like(scale)
    fields = jnp.stack([li, lj, hi, mid, low, zero, zero, zero]).astype(jnp.bfloat16)
    hot = source[:, None] == jnp.arange(128)[None, :]
    picks = jnp.stack([hot & (rank == 0)[:, None], hot & (rank == 1)[:, None]], axis=1)
    picks = picks.reshape(count, 256).astype(jnp.bfloat16)
    table = jnp.dot(fields, picks, preferred_element_type=jnp.float32)
    table = table.reshape(8, 2, 128)
    li, lj = table[0].astype(jnp.int32), table[1].astype(jnp.int32)
    first = lambda v: (v % 2) * 48 + (v // 2) * 3
    words = jnp.concatenate([first(li), first(lj), li, lj])
    scales = jnp.pad(table[2] + table[3] + table[4], ((0, 6), (0, 0)))
    return words, scales, source, rank


def meet_kernel(lq, rq, words_ref, scales_ref, trans_ref, lg, rg, rel_l, rel_r, got_ref, dr_ref,
                tf_ref, u_ref, w_ref, p_ref, pr_ref, q_ref, qr_ref, dl_ref, lhs_ref, out_ref, blk_ref, wv_ref, sv_ref, wt_ref, sc_ref,
                send, recv, osend, orecv, wsend, wrecv, ssend, srecv, loc):
    z, y, x, c = (lax.axis_index(n) for n in AXES)

    def dev(dz=0, dy=0, dx=0, dc=0):
        return (lax.rem(z + dz, 4), lax.rem(y + dy, 4), lax.rem(x + dx, 4), lax.rem(c + dc, 2))

    def plane(o):
        return dev(dy=lax.rem(o // 4, 4), dx=lax.rem(o, 4), dc=o // 16)

    def mirror(o):
        return (o // 16) * 16 + lax.rem(4 - lax.rem(o // 4, 4), 4) * 4 + lax.rem(4 - lax.rem(o, 4), 4)

    def remote(src, dst, a, b, to):
        return pltpu.make_async_remote_copy(
            src_ref=src, dst_ref=dst, send_sem=a, recv_sem=b, device_id=to, device_id_type=MESH)

    def out_copy(o):
        return remote(out_ref.at[o], got_ref.at[mirror(o)], osend.at[o], orecv.at[o], plane(o))

    def word_copy(o):
        return remote(words_ref, wv_ref.at[mirror(o)], wsend.at[o], wrecv.at[o], plane(o))

    def scale_copy(o):
        return remote(scales_ref, sv_ref.at[mirror(o)], ssend.at[o], srecv.at[o], plane(o))

    barrier = pltpu.get_barrier_semaphore()
    for o in range(1, 32):
        pl.semaphore_signal(barrier, inc=1, device_id=plane(jnp.int32(o)), device_id_type=MESH)
    for d in (1, 3):
        pl.semaphore_signal(barrier, inc=1, device_id=dev(dz=d), device_id_type=MESH)
    pl.semaphore_wait(barrier, 33)

    copies = {}

    def send_to(name, src, dst, to):
        i = len(copies)
        copy = remote(src, dst, send.at[i], recv.at[i], to)
        copy.start()
        copies[name] = copy

    got = lambda *names: [copies[n].wait_recv() for n in names]
    part = lambda d: lax.rem(x + d, 4)
    lo, hi = pl.ds(0, HALF), pl.ds(HALF, ROWS - HALF)
    lat = lambda dz, dx: ORDER[dx] * 4 + ORDER[dz]
    rat = lambda dc, dy, dx: dc * 16 + dy * 4 + dx

    def ring_l(dx):
        src = lq.at[x] if dx == 0 else lg.at[lat(0, dx)]
        send_to(("z+", dx), src, lg.at[lat(3, dx)], dev(dz=1))
        send_to(("z-", dx), src, lg.at[lat(1, dx)], dev(dz=3))

    def ring_r(dx):
        src = rq.at[x] if dx == 0 else rg.at[rat(0, 0, dx)]
        send_to(("y+", dx), src, rg.at[rat(0, 3, dx)], dev(dy=1))
        send_to(("y-", dx), src, rg.at[rat(0, 1, dx)], dev(dy=3))
        send_to(("c", 0, dx), src, rg.at[rat(1, 0, dx)], dev(dc=1))

    def relay(dl, dr):
        got(("z+", dl))
        send_to(("zr+", dl), lg.at[lat(3, dl), lo], lg.at[lat(2, dl), lo], dev(dz=1))
        got(("z-", dl))
        send_to(("zr-", dl), lg.at[lat(1, dl), hi], lg.at[lat(2, dl), hi], dev(dz=3))
        got(("y+", dr))
        send_to(("yr+", dr), rg.at[rat(0, 3, dr), lo], rg.at[rat(0, 2, dr), lo], dev(dy=1))
        send_to(("c", 3, dr), rg.at[rat(0, 3, dr)], rg.at[rat(1, 3, dr)], dev(dc=1))
        got(("y-", dr))
        send_to(("yr-", dr), rg.at[rat(0, 1, dr), hi], rg.at[rat(0, 2, dr), hi], dev(dy=3))
        send_to(("c", 1, dr), rg.at[rat(0, 1, dr)], rg.at[rat(1, 1, dr)], dev(dc=1))

    def last(dl, dr):
        got(("yr+", dr), ("yr-", dr))
        send_to(("c", 2, dr), rg.at[rat(0, 2, dr)], rg.at[rat(1, 2, dr)], dev(dc=1))
        got(("zr+", dl), ("zr-", dl))

    def product(src, weight, store, rest):
        lane = lax.broadcasted_iota(jnp.int32, (48, 128), 1)
        for e in range(2):
            own = (lane < 64) if e == 0 else (lane >= 64)
            lhs_ref[e * 832:e * 832 + 768, :128] = src[e * 768:(e + 1) * 768, :]
            for p in range(16):
                tail = (lane // 8) == (p % 8 + (8 if e == 0 else 0))
                x2 = src[PAIRED + 48 * p:PAIRED + 48 * p + 48, :]
                x3 = src[TAIL + 48 * (p // 8):TAIL + 48 * (p // 8) + 48, :]
                at = e * 832 + 48 * p
                lhs_ref[at:at + 48, 128:] = jnp.where(own, x2, jnp.where(tail, x3, jnp.zeros_like(x3)))
        for h in range(2):
            lhs_ref[768:832, 128 * h:128 * h + 128] = src[REM + 64 * h:REM + 64 * h + 64, :]
        first = jnp.dot(lhs_ref[:832, :], weight[0], preferred_element_type=jnp.float32)
        store(0, first[:768].reshape(48, 16, K))
        rest(first[768:])
        second = jnp.dot(lhs_ref[832:, :], weight[1], preferred_element_type=jnp.float32)
        store(48, second.reshape(48, 16, K))

    def load(src, k):
        return pltpu.make_async_copy(src, blk_ref.at[k], loc.at[k])

    def diagonal(main, rem, out, base, q, add):
        rows = tf_ref[pl.ds(pl.multiple_of(base + 48 * q, 8), 48), :]

        @pl.loop(0, 8)
        def _(t):
            for i in range(4):
                f = 4 * t + i
                group = (i % 2) * 48 + (2 * t + i // 2) * 3
                prod = main[pl.ds(group, 3)].reshape(48, K) * rows
                total = jnp.sum(prod, axis=0, keepdims=True)
                for r in range(2):
                    total += rem[pl.ds(2 * f + r, 1), :] * tf_ref[pl.ds(base + 192 + 2 * q + r, 1), :]
                if add:
                    total += out[pl.ds(f, 1), :]
                out[pl.ds(f, 1), :] = total

    def trailing():
        dr_ref[...] = jnp.zeros_like(dr_ref)

        @pl.loop(0, 4)
        def _(q):
            load(rq.at[q], 0).start()
            load(rq.at[q], 0).wait()

            def store(g, value):
                q_ref[g:g + 48] = value

            def rest(value):
                qr_ref[...] = value

            product(blk_ref.at[0], w_ref, store, rest)
            diagonal(q_ref, qr_ref, dr_ref, 200, q, True)

    def left(start, stop):
        load(lg.at[start], 0).start()

        @pl.loop(start, stop)
        def _(at):
            k = lax.rem(at - start, 2)

            @pl.when(at + 1 < stop)
            def _():
                load(lg.at[at + 1], 1 - k).start()

            load(lg.at[at], k).wait()

            def store(g, value):
                p_ref[at, g:g + 48] = value

            def rest(value):
                pr_ref[at] = value

            product(blk_ref.at[k], u_ref, store, rest)

            diagonal(p_ref.at[at], pr_ref.at[at], dl_ref.at[at], 0, x, False)

    send_to(("xl", 3), lq.at[part(1)], lg.at[lat(0, 3)], dev(dx=1))
    send_to(("xr", 1), rq.at[part(3)], rg.at[rat(0, 0, 1)], dev(dx=3))
    ring_l(0)
    ring_r(0)
    send_to(("xr", 3), rq.at[part(1)], rg.at[rat(0, 0, 3)], dev(dx=1))
    send_to(("xl", 1), lq.at[part(3)], lg.at[lat(0, 1)], dev(dx=3))
    send_to("l_rel", lq.at[part(2)], rel_l, dev(dx=1))
    send_to("r_rel", rq.at[part(2)], rel_r, dev(dx=3))

    @pl.loop(1, 32)
    def _(o):
        word_copy(o).start()
        scale_copy(o).start()

    wv_ref[0] = words_ref[...]
    sv_ref[0] = scales_ref[...]
    tf_ref[...] = jnp.zeros_like(tf_ref)
    tf_ref[:, :400] = trans_ref[...].astype(jnp.float32)
    for base, ref in ((0, u_ref), (200, w_ref)):
        tile = jnp.concatenate([tf_ref[base + 192:base + 200, :]] * 8).astype(jnp.bfloat16)
        half = tf_ref[base + 128:base + 192, :].astype(jnp.bfloat16)
        for e in range(2):
            ref[e, :128, :] = tf_ref[base:base + 128, :].astype(jnp.bfloat16)
            ref[e, 128 + 64 * e:192 + 64 * e, :] = half
            ref[e, 192 - 64 * e:256 - 64 * e, :] = tile
    for k, (src, dst) in enumerate([(lq, lg.at[lat(0, 0)]), (rq, rg.at[0])]):
        load(src.at[x], k).start()
        load(src.at[x], k).wait()
        out = pltpu.make_async_copy(blk_ref.at[k], dst, loc.at[2])
        out.start()
        out.wait()
    trailing()
    relay(0, 0)
    got(("xl", 3))
    ring_l(3)
    got(("xr", 1))
    ring_r(1)
    left(0, 2)
    last(0, 0)
    got(("xl", 1))
    ring_l(1)
    got(("xr", 3))
    ring_r(3)
    left(2, 4)
    relay(3, 1)
    left(4, 6)
    got("l_rel")
    send_to(("xl", 2), rel_l, lg.at[lat(0, 2)], dev(dx=1))
    got("r_rel")
    send_to(("xr", 2), rel_r, rg.at[rat(0, 0, 2)], dev(dx=3))
    last(3, 1)
    left(6, 9)
    relay(1, 3)
    got(("xl", 2))
    ring_l(2)
    got(("xr", 2))
    ring_r(2)
    left(9, 11)
    last(1, 3)
    left(11, 13)
    relay(2, 2)
    left(13, 15)
    last(2, 2)
    left(15, 16)
    for dx in range(4):
        for dy in range(4):
            copies[("c", dy, dx)].wait_recv()

    @pl.loop(1, 32)
    def _(o):
        word_copy(o).wait_recv()
        scale_copy(o).wait_recv()

    load(rg.at[31], 1).start()
    to_s = [pltpu.make_async_copy(wv_ref, wt_ref, loc.at[2]), pltpu.make_async_copy(sv_ref, sc_ref, loc.at[3])]
    for t in to_s:
        t.start()
    for t in to_s:
        t.wait()

    @pl.loop(0, 32)
    def _(step):
        o = 31 - step
        k = lax.rem(o, 2)

        @pl.when(o > 0)
        def _():
            load(rg.at[o - 1], 1 - k).start()

        load(rg.at[o], k).wait()

        def store(g, value):
            q_ref[g:g + 48] = value

        def rest(value):
            qr_ref[...] = value

        product(blk_ref.at[k], w_ref, store, rest)

        @pl.loop(0, 8)
        def _(t):
            for i in range(4):
                zs, xs, r = t // 2, lax.rem(t, 2) * 2 + i // 2, i % 2
                lane = ((zs * 4 + y) * 4 + xs) * 2 + c
                gi, gj, li, lj = (wt_ref[o, 2 * m + r, lane] for m in range(4))
                dz, dx = lax.rem(zs - z + 4, 4), lax.rem(xs - x + 4, 4)
                s = (lax.rem(dx, 3) + 1) * ((dx + 3) // 4) * 4 + (lax.rem(dz, 3) + 1) * ((dz + 3) // 4)
                prod = p_ref[s, pl.ds(gi, 3)] * q_ref[pl.ds(gj, 3)]
                total = jnp.sum(prod.reshape(48, K), axis=0, keepdims=True)
                for m in range(2):
                    total += pr_ref[s, pl.ds(2 * li + m, 1), :] * qr_ref[pl.ds(2 * lj + m, 1), :]
                out_ref[o, pl.ds(4 * t + i, 1), :] = total * sc_ref[o, r, lane] + dl_ref[s, pl.ds(li, 1), :]

        @pl.when(o > 0)
        def _():
            out_copy(o).start()

    own = pltpu.make_async_copy(out_ref.at[0], got_ref.at[0], loc.at[2])
    own.start()
    own.wait()
    for copy in copies.values():
        copy.wait_send()
    assert len(copies) == NCOPY

    @pl.loop(1, 32)
    def _(o):
        word_copy(o).wait_send()
        scale_copy(o).wait_send()
        out_copy(o).wait_recv()
        out_copy(o).wait_send()


def meet(lq, rq, words, scales, transform):
    blk = (ROWS, 128)
    any_ = pl.BlockSpec(memory_space=pl.ANY)
    vmem = pl.BlockSpec(memory_space=pltpu.VMEM)
    bf, f32 = jnp.bfloat16, jnp.float32
    dma = lambda n: pltpu.SemaphoreType.DMA((n,))
    out = jax.ShapeDtypeStruct
    return pl.pallas_call(
        meet_kernel,
        out_shape=(out((16,) + blk, bf), out((32,) + blk, bf), out(blk, bf), out(blk, bf), out((32, 32, K), f32),
                   out((32, K), f32)),
        in_specs=[any_, any_] + [vmem] * 3,
        out_specs=(any_,) * 5 + (vmem,),
        scratch_shapes=[
            pltpu.VMEM((400, K), f32), pltpu.VMEM((2, 256, K), bf), pltpu.VMEM((2, 256, K), bf),
            pltpu.VMEM((16, 96, 16, K), f32), pltpu.VMEM((16, 64, K), f32),
            pltpu.VMEM((96, 16, K), f32), pltpu.VMEM((64, K), f32),
            pltpu.VMEM((16, 32, K), f32), pltpu.VMEM((1600, 256), bf),
            pltpu.VMEM((32, 32, K), f32), pltpu.VMEM((2,) + blk, bf),
            pltpu.VMEM((32, 8, 128), jnp.int32), pltpu.VMEM((32, 8, 128), f32),
            pltpu.SMEM((32, 8, 128), jnp.int32), pltpu.SMEM((32, 8, 128), f32),
            dma(NCOPY), dma(NCOPY), dma(32), dma(32), dma(32), dma(32), dma(32), dma(32), dma(4),
        ],
        compiler_params=pltpu.CompilerParams(collective_id=0, has_side_effects=True, vmem_limit_bytes=67043328),
        name="meet",
    )(lq, rq, words, scales, transform)[4:]


def finish_kernel(where, got_ref, dr_ref, en_ref, sum_ref, part_ref, inbox_ref, send, recv):
    z, y, x, c = (lax.axis_index(n) for n in AXES)

    def dev(dz=0, dy=0, dx=0, dc=0):
        return (lax.rem(z + dz, 4), lax.rem(y + dy, 4), lax.rem(x + dx, 4), lax.rem(c + dc, 2))

    barrier = pltpu.get_barrier_semaphore()
    partners = [dev(**{k: d}) for k in ("dx", "dy", "dz") for d in (1, 2, 3)] + [dev(dc=1)]
    for p in partners:
        pl.semaphore_signal(barrier, inc=1, device_id=p, device_id_type=MESH)
    pl.semaphore_wait(barrier, len(partners))
    copies = []

    def send_to(src, dst, to):
        i = len(copies)
        copy = pltpu.make_async_remote_copy(
            src_ref=src, dst_ref=dst, send_sem=send.at[i], recv_sem=recv.at[i],
            device_id=to, device_id_type=MESH)
        copy.start()
        copies.append(copy)
        return copy

    me = ((z * 4 + y) * 4 + x) * 2 + c

    @pl.loop(0, 16)
    def _(t):
        for i in range(8):
            d = 8 * t + i
            dc, dy, n, lj = where[0, d], where[1, d], where[2, d], where[3, d]
            row = dr_ref[pl.ds(lj, 1), :]
            for dx in range(4):
                row += got_ref[dc, dy, dx, pl.ds(n, 1), :]
            en_ref[pl.ds(d, 1), :] = row[:, :400]

    value = en_ref[...]
    mean = jnp.sum(value * value, axis=1, keepdims=True) * jnp.float32(1.0 / 400.0)
    index = (me * 128 + lax.broadcasted_iota(jnp.int32, (128, 1), 0)).astype(jnp.float32)
    total = jnp.sum((index + 1.0) * jnp.float32(1.0 / 16384.0) * mean, axis=0, keepdims=True)
    total = jnp.broadcast_to(total * jnp.float32(2.0 / 16384.0), (8, 128))
    stages = [[dict(dx=d) for d in (1, 2, 3)], [dict(dy=d) for d in (1, 2, 3)], [dict(dz=d) for d in (1, 2, 3)], [dict(dc=1)]]
    slot = 0
    for k, stage in enumerate(stages):
        part_ref[k] = total
        sent = []
        for j, to in enumerate(stage):
            sent.append((slot, send_to(part_ref.at[k], inbox_ref.at[slot], dev(**to))))
            slot += 1
        for at, copy in sent:
            copy.wait_recv()
        values = [total] + [inbox_ref[at] for at, _ in sent]
        if len(values) == 4:
            total = (values[0] + values[2]) + (values[1] + values[3])
        else:
            total = values[0] + values[1]
    sum_ref[...] = total
    for copy in copies:
        copy.wait_send()


def finish(where, parts, dr):
    n = 10
    vmem = pl.BlockSpec(memory_space=pltpu.VMEM)
    return pl.pallas_call(
        finish_kernel,
        out_shape=(jax.ShapeDtypeStruct((128, 400), jnp.float32), jax.ShapeDtypeStruct((8, 128), jnp.float32)),
        in_specs=[pl.BlockSpec(memory_space=pltpu.SMEM), vmem, vmem],
        out_specs=(vmem, vmem),
        scratch_shapes=[
            pltpu.VMEM((4, 8, 128), jnp.float32),
            pltpu.VMEM((10, 8, 128), jnp.float32), pltpu.SemaphoreType.DMA((n,)),
            pltpu.SemaphoreType.DMA((n,)),
        ],
        compiler_params=pltpu.CompilerParams(collective_id=1, has_side_effects=True, vmem_limit_bytes=32 << 20),
        name="finish",
    )(where, parts.reshape(2, 4, 4, 32, K), dr)


def local(potentials, dimers, coupling, transform):
    z, y, x, c = (lax.axis_index(n) for n in AXES)
    words, scales, source, rank = slot_table(dimers, coupling)
    lq, rq = pack(potentials)

    parts, dr = meet(lq, rq, words, scales, transform)
    zs, ys, xs, cs = source // 32, (source // 8) % 4, (source // 2) % 4, source % 2
    where = jnp.stack([(cs - c) % 2, (ys - y) % 4, (zs * 4 + xs) * 2 + rank, dimers[:, 1] % 32])
    energies, total = finish(where, parts, dr)
    return energies, total[0, :1]


def solution(mesh):
    split = Mesh(mesh.devices.reshape(4, 4, 4, mesh.shape["sub"]), AXES)
    return jax.shard_map(
        local,
        mesh=split,
        in_specs=(P(AXES, None, None), P(AXES, None), P(AXES), P()),
        out_specs=(P(AXES, None), P()),
        check_vma=False,
    )
```

time: 228 us -> 214 us (0.939)
  Pallas kernels: 206 us -> 198 us
  matrix products: 4.24 us -> 0.14 us
  other arithmetic: 8.49 us -> 5.03 us
    pallas_call x2 -> x1, Pallas kernels: 184 us -> 175 us  [meet(): pl.pallas_call(meet_kernel, out_shape=(out((16,) + blk, bf), out((32,) +...]
    dot_general x1 -> x0, matrix products: 4.11 us -> none  [local(): jnp.einsum('fab,bk->fak', potentials, lower, preferred_element_type=jnp.f...]
    unnamed x17 -> x13, local copies, waits for them, and re-layouts: 5.69 us -> 8.7 us
where the time goes in v3:
time: 214 us
  Pallas kernels  198 us (93%)
  local copies, waits for them, and re-layouts  9.84 us (5%)
  other arithmetic  5.03 us (2%)
    pallas_call x1, Pallas kernels, meet(): pl.pallas_call(meet_kernel, out_shape=(out((16,) + blk, bf), out((32,) +...  175 us
    pallas_call x1, Pallas kernels, finish(): pl.pallas_call(finish_kernel, out_shape=(jax.ShapeDtypeStruct((128, 400),...  16.7 us
    unnamed x13, local copies, waits for them, and re-layouts  8.7 us
    pallas_call x1, Pallas kernels, pack(): pl.pallas_call(pack_kernel, out_shape=(shape, shape), in_specs=[vmem, vme...  5.79 us

profile of v3, /device:TPU:1, one launch (start us, length us, event | category | flops | bytes accessed | tf_op | source)
XLA Modules:
  0.0 213.7 jit_solution(4373961385321635377)
XLA Ops:
  0.6 0.7 fusion.26
  1.3 0.7 and_select_fusion.10
  2.0 0.2 select_reduce_fusion
  2.2 0.7 fusion.20
  2.9 0.8 and_select_fusion.18
  3.7 0.5 pad_add_fusion.2.where
  4.3 0.7 fusion.16
  5.0 0.1 fusion.27
  5.2 0.6 pad_add_fusion.1.words_ref
  5.8 0.6 pad.4.scales_ref
  6.4 0.1 fusion.perm_ref
  6.5 0.0 copy-start
  6.5 1.9 copy-done
  8.4 5.8 %pack.1 = (bf16[4,2528,128]{2,1,0:T(8,128)(2,1)S(1)}, bf16[4,2528,128]{2,1,0:T(8,128)(2,1)S(1)}) custom-call(bf16[32,200,200]{2,1,0:T(8,128)(2,1)S(1)} %copy-done, bf16[256,256]{1,0:T(8,128)(2,1)S(1)} %fusion.perm_ref), custom_call_target="tpu_custom_call" | custom-call | tf_op jit(solution)/shard_map/pack/pallas_call | solution.py:72
  14.2 0.0 copy-start.1
  14.2 1.4 copy-done.1
  15.7 0.0 copy-start.2
  15.7 1.5 copy-done.2
  17.1 175.4 %meet.1 = (bf16[16,2528,128]{2,1,0:T(8,128)(2,1)}, bf16[32,2528,128]{2,1,0:T(8,128)(2,1)}, bf16[2528,128]{1,0:T(8,128)(2,1)}, bf16[2528,128]{1,0:T(8,128)(2,1)},...) custom-call(bf16[4,2528,128]{2,1,0:T(8,128)(2,1)} %copy-done.1, bf16[4,2528,128]{2,1,0:T(8,128)(2,1)} %copy-done.2, ...), custom_call_target="tpu_custom_call" | custom-call | tf_op jit(solution)/shard_map/meet/pallas_call | solution.py:402
  192.6 0.0 copy-start.3
  192.6 1.6 copy-done.3
  194.2 0.0 copy-start.4
  194.2 0.8 copy-done.4
  195.0 0.0 copy-start.5
  195.0 0.6 copy-done.5
  195.6 16.7 %finish.1 = (f32[128,400]{1,0:T(8,128)S(1)}, f32[8,128]{1,0:T(8,128)S(1)}) custom-call(s32[4,128]{1,0:T(4,128)S(1)} %copy-done.5, f32[2,4,4,32,512]{4,3,2,1,0:T(8,128)S(1)} %bitcast.42, f32[32,512]{1,0:T(8,128)S(1)} %copy-done.4), custom_call_target="tpu_custom_call" | custom-call | tf_op jit(solution)/shard_map/finish/pallas_call | solution.py:485
  212.3 0.5 slice.38
  212.8 0.8 copy.8
  (10 shorter events, 0.1 us)
Async XLA Ops:
  6.5 1.9 copy-start
  14.2 1.5 copy-start.1
  15.7 1.5 copy-start.2
  192.6 1.6 copy-start.3
  194.2 0.8 copy-start.4
  195.0 0.6 copy-start.5
